TPU v7x, 32 devices: a whole 2x2x4 slice. The times are simulated.
32 devices in a mesh: seq: 8 (over y, x, core), grp: 4 (over z).
Axes of the slice: x: 2, y: 2, z: 4, core: 2. Of those that a mesh axis runs over, the one named last changes fastest.
Arguments:
- queries: bfloat16 [8192, 4096], P(('grp', 'seq')), parts along dimension 0, may hold values from -64 to 64
- keys: bfloat16 [8192, 1024], P(('grp', 'seq')), parts along dimension 0, may hold values from -64 to 64
- values: bfloat16 [8192, 1024], P(('grp', 'seq')), parts along dimension 0, may hold values from -6 to 6
- doc_lengths: int32 [24], P('grp'), parts along dimension 0, may hold values from 1 to 8, 16 in all
Outputs:
- attended: bfloat16 [8192, 4096], P(('grp', 'seq')), parts along dimension 0
There are 4 independent parts, one for each index of `grp`. A program takes and returns all parts, laid end to end along the dimension named above; each array names one. Nothing has to cross between parts.
Inputs may be any that keep to these rules, and one draw needn't show every extreme that they name: `doc_lengths`: lengths of the documents in units of 128 tokens, summing to 16.
All inputs are finite; a program needn't handle non-finite values.
Results may differ from a plain program's by a relative error of at most 0.004.
Values may be sent and summed in bfloat16 or wider, within the bound.
No kernel may reach another device: no remote copies, remote signals or barrier semaphores. Data moves between devices by JAX's collectives and lax.ppermute only.
A program may use at most 128 MiB of HBM per device.

v0:
```python
import functools
import math

import jax
import jax.numpy as jnp
import numpy as np
from jax import lax
from jax.experimental import pallas as pl
from jax.experimental.pallas import tpu as pltpu
from jax.sharding import PartitionSpec as P


HEAD_DIM = 128
DOC_UNIT = 128
MOST_UNITS = 8
PARTS_OF_HEADS = 2


class Piece:
    def __init__(self, array, units):
        self.array, self.units = array, units

    def rows(self, first, last):
        return Piece(self.array[first * DOC_UNIT : last * DOC_UNIT], self.units[:, first:last])

    def to(self, pairs):
        units = np.full_like(self.units, -1)
        for source, target in pairs:
            units[target] = self.units[source]
        return Piece(lax.ppermute(self.array, "seq", pairs), units)


def cube_exchange(low, high):
    chip = lambda c, b: 2 * c + b
    both = (0, 1)
    swap = lambda *chips: [(chip(c, b), chip(c, 1 - b)) for c in chips for b in both]
    next_chip = [(chip(c, b), chip(c + 1, b)) for c in (0, 2) for b in both]
    beside = [(chip(c, 0), chip(c, 1)) for c in range(4)]
    a_low = low.to([(chip(1, 1), chip(3, 0))])
    a_high = high.to([(chip(1, b), chip(3, b)) for b in both])
    b_low = low.to([(chip(0, 1), chip(2, 0)), (chip(1, 0), chip(2, 1))])
    b_high = high.to([(chip(0, b), chip(2, b)) for b in both])
    near_low, near_high = low.to(next_chip), high.to(next_chip)
    on_low = a_low.to([(chip(3, 0), chip(2, 0))])
    on_high = a_high.to([(chip(3, b), chip(2, b)) for b in both])
    first = [
        low,
        high,
        low.to(beside),
        high.to(beside),
        a_low,
        a_high,
        b_low,
        b_high,
        near_low,
        on_low,
        near_low.to(swap(1, 3)),
        on_low.to([(chip(2, 0), chip(2, 1))]),
        b_low.to([(chip(2, 1), chip(2, 0))]),
        b_high.to([(chip(2, 1), chip(2, 0))]),
        a_high.to([(chip(3, 1), chip(3, 0))]),
    ]
    last = [near_high, on_high, near_high.to(swap(1, 3)), on_high.to(swap(2))]
    return first, last


def gather_exchange(own):
    count, each = own.units.shape
    everything = lax.all_gather(own.array, "seq", axis=0, tiled=True)
    return [Piece(everything, np.tile(np.arange(count * each), (count, 1)))]


def slots_of(pieces, window, each, wanted=lambda device, unit: True):
    slots, table = [], []
    count = pieces[0].units.shape[0]
    held = [set() for _ in range(count)]
    for number, piece in enumerate(pieces):
        for block in range(piece.units.shape[1]):
            column = []
            for device in range(count):
                unit = int(piece.units[device, block])
                last = each * device + each - 1
                fits = last - window < unit <= last and unit >= 0 and unit not in held[device]
                column.append(unit if fits else -1)
                if fits:
                    held[device].add(unit)
            if max(column) >= 0:
                slots.append((number, block))
                table.append(column)
    for device in range(count):
        last = each * device + each - 1
        units = range(max(0, last - window + 1), last + 1)
        assert held[device] == {unit for unit in units if wanted(device, unit)}
    return slots, np.array(table, np.int32).T


def doc_start(docs_ref, unit):
    start, passed = jnp.int32(0), jnp.int32(0)
    for d in range(docs_ref.shape[0]):
        passed = passed + docs_ref[d]
        start = jnp.where(passed <= unit, passed, start)
    return start


def held_unit(column, device):
    held = set(column.tolist()) - {-1}
    if len(held) == 1 and (column >= 0).all():
        return jnp.int32(held.pop())
    unit = jnp.int32(-1)
    for holder in np.flatnonzero(column >= 0):
        unit = jnp.where(device == int(holder), int(column[holder]), unit)
    return unit


FACTOR = HEAD_DIM**-0.5 * math.log2(math.e)


def rows_of(first, units):
    return pl.ds(pl.multiple_of(first * DOC_UNIT, DOC_UNIT), units * DOC_UNIT)


def columns_of(head, width=HEAD_DIM):
    return pl.ds(pl.multiple_of(head * width, width), width)


def stacked(q, heads):
    return jnp.concatenate([q[:, g * HEAD_DIM : (g + 1) * HEAD_DIM] for g in heads], axis=0)


def scores_of(q, key_rows):
    return lax.dot_general(
        q, key_rows, (((1,), (1,)), ((), ())), preferred_element_type=jnp.float32
    )


def mixed(weights, value_rows):
    ones = jnp.ones(value_rows.shape, value_rows.dtype)
    return jnp.dot(
        weights.astype(value_rows.dtype),
        jnp.concatenate([value_rows, ones], axis=1),
        preferred_element_type=jnp.float32,
    )


def masked_last(scores, units):
    last = scores[:, (units - 1) * DOC_UNIT :]
    row = lax.broadcasted_iota(jnp.int32, last.shape, 0) % DOC_UNIT
    column = lax.broadcasted_iota(jnp.int32, last.shape, 1)
    last = jnp.where(column <= row, last, -jnp.inf)
    if units == 1:
        return last
    return jnp.concatenate([scores[:, : (units - 1) * DOC_UNIT], last], axis=1)


def twice(tile):
    return jnp.concatenate([tile, tile], axis=1)


def in_turn(jobs, start, finish):
    pending = start(jobs[0])
    for number, job in enumerate(jobs):
        started = pending
        if number + 1 < len(jobs):
            pending = start(jobs[number + 1])
        finish(job, started)


CHUNK = 2
AT_ONCE = 2


def unit_copies(pieces, slots, table, sems, buf, device, lowest, place):
    def each_copy(act):
        for t, (number, block) in enumerate(slots):
            unit = held_unit(table[:, t], device)

            @pl.when(unit >= lowest)
            def _():
                act(
                    pltpu.make_async_copy(
                        pieces[number].at[pl.ds(block * DOC_UNIT, DOC_UNIT)],
                        buf.at[rows_of(place(unit), 1)],
                        sems.at[t],
                    )
                )

    return each_copy


def late_units(device):
    chip = device >> 1
    return 4 * chip - 3, 4 * chip - 1


def first_kernel(plan, docs_ref, q_hbm, *refs):
    slots, table, n_pieces, window, each, group, heads = plan
    pieces = refs[:n_pieces]
    mixed_ref, top_ref, q_all, buf, sems, q_sem = refs[n_pieces:]
    device = lax.axis_index("seq")
    first_unit = device * each
    base = first_unit + each - window
    late = late_units(device)
    columns = group * HEAD_DIM

    def place(unit):
        return unit - base - (unit > late[0]).astype(jnp.int32) - (unit > late[1]).astype(jnp.int32)

    each_copy = unit_copies(
        pieces, slots, table, sems, buf, device, doc_start(docs_ref, first_unit), place
    )
    q_copy = pltpu.make_async_copy(q_hbm, q_all, q_sem)
    each_copy(lambda copy: copy.start())
    q_copy.start()
    each_copy(lambda copy: copy.wait())
    q_copy.wait()

    def one_step(step, carry):
        pair, part = lax.div(step, each), lax.rem(step, each)
        unit = first_unit + part
        start = doc_start(docs_ref, unit)
        skipped = sum(((u >= start) & (u <= unit)).astype(jnp.int32) for u in late)
        here = unit - start + 1 - skipped
        for units in range(1, window - each):

            @pl.when(here == units)
            def _():
                rows = rows_of(place(unit) - units + 1, units)
                jobs = [(h, g) for h in range(AT_ONCE) for g in range(0, group, CHUNK)]

                def begin(job):
                    head, g = pair * AT_ONCE + job[0], job[1]
                    q = q_all[rows_of(part, 1), columns_of(head, columns)]
                    keys = buf[rows, columns_of(head)]
                    return scores_of(stacked(q, range(g, g + CHUNK)), keys)

                def end(job, scores):
                    h, g = job
                    head = pair * AT_ONCE + h
                    scores = masked_last(scores, units)
                    top = jnp.max(scores, axis=1, keepdims=True)
                    weights = jnp.exp2((scores - top) * FACTOR)
                    mine = pl.ds(g * DOC_UNIT, CHUNK * DOC_UNIT)
                    mixed_ref[step, h, mine] = mixed(weights, buf[rows, columns_of(heads + head)])
                    top_ref[step, h, mine] = jnp.broadcast_to(top, (CHUNK * DOC_UNIT, HEAD_DIM))

                in_turn(jobs, begin, end)

        return carry

    lax.fori_loop(0, heads // AT_ONCE * each, one_step, 0)


def last_kernel(plan, docs_ref, q_hbm, mixed_ref, top_ref, *refs):
    slots, table, n_pieces, _, each, group, heads = plan
    pieces = refs[:n_pieces]
    out_hbm, q_all, buf, out_all, sems, q_sem, out_sems = refs[n_pieces:]
    device = lax.axis_index("seq")
    first_unit = device * each
    late = late_units(device)
    columns = group * HEAD_DIM
    steps = heads // AT_ONCE * each

    place = lambda unit: (unit > late[0]).astype(jnp.int32)
    each_copy = unit_copies(pieces, slots, table, sems, buf, device, 0, place)
    q_copy = pltpu.make_async_copy(q_hbm, q_all, q_sem)

    def copy_out(pair):
        there = columns_of(pair, AT_ONCE * columns)
        return pltpu.make_async_copy(out_all.at[:, there], out_hbm.at[:, there], out_sems.at[pair])

    each_copy(lambda copy: copy.start())
    q_copy.start()
    each_copy(lambda copy: copy.wait())
    q_copy.wait()

    def one_step(step, carry):
        pair, part = lax.div(step, each), lax.rem(step, each)
        unit = first_unit + part
        start = doc_start(docs_ref, unit)
        count = sum((u >= start).astype(jnp.int32) for u in late)
        jobs = [(h, g) for h in range(AT_ONCE) for g in range(0, group, CHUNK)]

        def older(ref, job):
            return ref[step, job[0], pl.ds(job[1] * DOC_UNIT, CHUNK * DOC_UNIT)]

        def mean(result):
            return result[:, :HEAD_DIM] / result[:, HEAD_DIM:]

        def store(job, rows):
            for k in range(CHUNK):
                head = (pair * AT_ONCE + job[0]) * group + job[1] + k
                out_all[rows_of(part, 1), columns_of(head)] = rows[
                    k * DOC_UNIT : (k + 1) * DOC_UNIT
                ].astype(out_all.dtype)

        @pl.when(count == 0)
        def _():
            for job in jobs:
                store(job, mean(older(mixed_ref, job)))

        @pl.when(count > 0)
        def _():
            def begin(job):
                head = pair * AT_ONCE + job[0]
                q = q_all[rows_of(part, 1), columns_of(head, columns)]
                return scores_of(stacked(q, range(job[1], job[1] + CHUNK)), buf[:, columns_of(head)])

            def end(job, scores):
                head = pair * AT_ONCE + job[0]
                column = lax.broadcasted_iota(jnp.int32, scores.shape, 1)
                scores = jnp.where(column >= (2 - count) * DOC_UNIT, scores, -jnp.inf)
                old = older(top_ref, job)
                top = jnp.maximum(old, jnp.max(scores, axis=1, keepdims=True))
                weights = jnp.exp2((scores - twice(top)) * FACTOR)
                shrink = jnp.exp2((old - top) * FACTOR)
                result = mixed(weights, buf[:, columns_of(heads + head)])
                store(job, mean(older(mixed_ref, job) * twice(shrink) + result))

            in_turn(jobs, begin, end)

        @pl.when(part == each - 1)
        def _():
            copy_out(pair).start()

        return carry

    lax.fori_loop(0, steps, one_step, 0)
    for pair in range(heads // AT_ONCE):
        copy_out(pair).wait()


def in_two(queries, doc_lengths, first, last, window, each, group, heads):
    rows = each * DOC_UNIT
    dtype = queries.dtype
    steps = heads // AT_ONCE * each
    anywhere = pl.BlockSpec(memory_space=pl.ANY)
    dma = pltpu.SemaphoreType.DMA
    tile = (steps, AT_ONCE, group * DOC_UNIT, HEAD_DIM)
    state = (
        pltpu.VMEM((*tile[:-1], 2 * HEAD_DIM), jnp.float32),
        pltpu.VMEM(tile, jnp.float32),
    )
    on_chip = pl.BlockSpec(memory_space=pltpu.VMEM)
    is_late = lambda device, unit: unit in late_units(device)

    def call(kernel, pieces, wanted, held_rows, operands, in_specs, shapes, out_specs, scratch):
        slots, table = slots_of(pieces, window, each, wanted)
        plan = (slots, table, len(pieces), window, each, group, heads)
        scratch = [
            pltpu.VMEM(queries.shape, dtype),
            pltpu.VMEM((held_rows, 2 * heads * HEAD_DIM), dtype),
            *scratch(len(slots)),
        ]
        work = held_rows * rows * heads * group * HEAD_DIM * 2
        return pl.pallas_call(
            functools.partial(kernel, plan),
            out_shape=shapes,
            grid_spec=pltpu.PrefetchScalarGridSpec(
                num_scalar_prefetch=1,
                grid=(),
                in_specs=[*in_specs, *[anywhere] * len(pieces)],
                out_specs=out_specs,
                scratch_shapes=scratch,
            ),
            compiler_params=pltpu.CompilerParams(vmem_limit_bytes=VMEM_LIMIT),
            cost_estimate=pl.CostEstimate(
                flops=work, transcendentals=work // (4 * HEAD_DIM), bytes_accessed=4 * queries.size * 2
            ),
        )(doc_lengths, *operands, *[p.array for p in pieces])

    so_far = call(
        first_kernel,
        first,
        lambda device, unit: not is_late(device, unit),
        (window - 2) * DOC_UNIT,
        (queries,),
        (anywhere,),
        state,
        (on_chip, on_chip),
        lambda n: [dma((n,)), dma],
    )
    return call(
        last_kernel,
        last,
        is_late,
        2 * DOC_UNIT,
        (queries, *so_far),
        (anywhere, on_chip, on_chip),
        jax.ShapeDtypeStruct(queries.shape, dtype),
        anywhere,
        lambda n: [pltpu.VMEM(queries.shape, dtype), dma((n,)), dma, dma((heads // AT_ONCE,))],
    )


VMEM_LIMIT = 24 << 20


def attend_kernel(plan, docs_ref, q_hbm, *refs):
    slots, table, n_pieces, window, each, group, first_head, heads, n_docs = plan
    pieces, out_hbm = refs[:n_pieces], refs[-9]
    q_all, out_all, buf, sems, q_sems, out_sems, state_m, state_o = refs[-8:]
    device = lax.axis_index("seq")
    first_unit = device * each
    base = first_unit + each - window
    width = heads * HEAD_DIM
    columns = group * HEAD_DIM

    def doc_start(unit):
        start, passed = jnp.int32(0), jnp.int32(0)
        for d in range(n_docs):
            passed = passed + docs_ref[d]
            start = jnp.where(passed <= unit, passed, start)
        return start

    lowest_unit = doc_start(first_unit)

    def each_copy(act):
        for t, (number, block) in enumerate(slots):
            held = set(table[:, t].tolist()) - {-1}
            if len(held) == 1:
                unit = jnp.int32(held.pop())
            else:
                unit = jnp.int32(-1)
                for holder in np.flatnonzero(table[:, t] >= 0):
                    unit = jnp.where(device == int(holder), int(table[holder, t]), unit)

            @pl.when((unit >= lowest_unit) & (unit < first_unit + each))
            def _():
                place = pl.multiple_of((unit - base) * DOC_UNIT, DOC_UNIT)
                act(
                    pltpu.make_async_copy(
                        pieces[number].at[pl.ds(block * DOC_UNIT, DOC_UNIT)],
                        buf.at[pl.ds(place, DOC_UNIT)],
                        sems.at[t],
                    )
                )

    def q_copy(head):
        there = pl.ds(pl.multiple_of((first_head + head) * columns, columns), columns)
        return pltpu.make_async_copy(q_hbm.at[:, there], q_all.at[head], q_sems.at[head])

    def out_copy(head):
        there = pl.ds(pl.multiple_of((first_head + head) * columns, columns), columns)
        return pltpu.make_async_copy(out_all.at[head], out_hbm.at[:, there], out_sems.at[head])

    q_copy(0).start()
    each_copy(lambda copy: copy.start())
    for head in range(1, heads):
        q_copy(head).start()
    each_copy(lambda copy: copy.wait())

    factor = HEAD_DIM**-0.5 * math.log2(math.e)
    ones = jnp.ones((min(MOST_UNITS, window) * DOC_UNIT, HEAD_DIM), buf.dtype)
    most = min(MOST_UNITS, window - each + 1)
    longer = window - each + 1 > most

    def each_head(head, carry):
        q_copy(head).wait()
        key_columns = pl.ds(pl.multiple_of(head * HEAD_DIM, HEAD_DIM), HEAD_DIM)
        value_columns = pl.ds(pl.multiple_of(width + head * HEAD_DIM, HEAD_DIM), HEAD_DIM)

        def stacked(part):
            q = q_all[head, pl.ds(part * DOC_UNIT, DOC_UNIT), :]
            return jnp.concatenate(
                [q[:, g * HEAD_DIM : (g + 1) * HEAD_DIM] for g in range(group)], axis=0
            )

        def scores_of(q, first, units):
            there = pl.ds(pl.multiple_of(first * DOC_UNIT, DOC_UNIT), units * DOC_UNIT)
            return lax.dot_general(
                q, buf[there, key_columns], (((1,), (1,)), ((), ())), preferred_element_type=jnp.float32
            )

        def mixed(weights, first, units):
            there = pl.ds(pl.multiple_of(first * DOC_UNIT, DOC_UNIT), units * DOC_UNIT)
            value_rows = jnp.concatenate([buf[there, value_columns], ones[: units * DOC_UNIT]], axis=1)
            return jnp.dot(
                weights.astype(buf.dtype), value_rows, preferred_element_type=jnp.float32
            )

        def store(part, result):
            result = result[:, :HEAD_DIM] / result[:, HEAD_DIM:]
            for g in range(group):
                out_all[
                    head, pl.ds(part * DOC_UNIT, DOC_UNIT), g * HEAD_DIM : (g + 1) * HEAD_DIM
                ] = result[g * DOC_UNIT : (g + 1) * DOC_UNIT].astype(out_all.dtype)

        for part in range(each):
            unit = first_unit + part
            start = doc_start(unit)
            count = unit - start + 1
            here = lax.rem(count - 1, most) + 1
            for units in range(1, most + 1):

                @pl.when(here == units)
                def _():
                    first = unit - base - units + 1
                    scores = scores_of(stacked(part), first, units)
                    last = scores[:, (units - 1) * DOC_UNIT :]
                    row = lax.broadcasted_iota(jnp.int32, last.shape, 0) % DOC_UNIT
                    column = lax.broadcasted_iota(jnp.int32, last.shape, 1)
                    last = jnp.where(column <= row, last, -jnp.inf)
                    if units > 1:
                        before = scores[:, : (units - 1) * DOC_UNIT]
                        scores = jnp.concatenate([before, last], axis=1)
                    else:
                        scores = last
                    top = jnp.max(scores, axis=1, keepdims=True)
                    result = mixed(jnp.exp2((scores - top) * factor), first, units)
                    if longer:
                        state_m[...], state_o[...] = top, result
                    else:
                        store(part, result)

            if longer:

                def add_block(number, carry):
                    first = start - base + number * most
                    scores = scores_of(stacked(part), first, most)
                    old = state_m[...]
                    top = jnp.maximum(old, jnp.max(scores, axis=1, keepdims=True))
                    weights = jnp.exp2((scores - top) * factor)
                    shrink = jnp.exp2((old - top) * factor)
                    state_m[...] = top
                    state_o[...] = state_o[...] * shrink + mixed(weights, first, most)
                    return carry

                lax.fori_loop(0, lax.div(count - 1, most), add_block, 0)
                store(part, state_o[...])
        out_copy(head).start()
        return carry

    lax.fori_loop(0, heads, each_head, 0)
    for head in range(heads):
        out_copy(head).wait()


def attend(queries, doc_lengths, pieces, window, each, group, first_head, heads, before):
    slots, table = slots_of(pieces, window, each)
    width = heads * HEAD_DIM
    rows = each * DOC_UNIT
    columns = group * HEAD_DIM
    plan = (slots, table, len(pieces), window, each, group, first_head, heads, doc_lengths.shape[0])
    anywhere = pl.BlockSpec(memory_space=pl.ANY)
    extra = [] if before is None else [before]
    work = window * DOC_UNIT * rows * heads * group * HEAD_DIM * 2
    n_long = group * DOC_UNIT if window - each + 1 > MOST_UNITS else 8
    held = (window * DOC_UNIT * 2 * width + 2 * rows * columns * heads) * 2
    return pl.pallas_call(
        functools.partial(attend_kernel, plan),
        out_shape=jax.ShapeDtypeStruct(queries.shape, queries.dtype),
        grid_spec=pltpu.PrefetchScalarGridSpec(
            num_scalar_prefetch=1,
            grid=(),
            in_specs=[anywhere] * (1 + len(pieces) + len(extra)),
            out_specs=anywhere,
            scratch_shapes=[
                pltpu.VMEM((heads, rows, columns), queries.dtype),
                pltpu.VMEM((heads, rows, columns), queries.dtype),
                pltpu.VMEM((window * DOC_UNIT, 2 * width), queries.dtype),
                pltpu.SemaphoreType.DMA((len(slots),)),
                pltpu.SemaphoreType.DMA((heads,)),
                pltpu.SemaphoreType.DMA((heads,)),
                pltpu.VMEM((n_long, 1), jnp.float32),
                pltpu.VMEM((n_long, 2 * HEAD_DIM), jnp.float32),
            ],
        ),
        input_output_aliases={} if before is None else {2 + len(pieces): 0},
        compiler_params=pltpu.CompilerParams(vmem_limit_bytes=held + (12 << 20)),
        cost_estimate=pl.CostEstimate(
            flops=work,
            transcendentals=work // (4 * HEAD_DIM),
            bytes_accessed=2 * rows * columns * heads * 2 + window * DOC_UNIT * width * 4,
        ),
    )(doc_lengths, queries, *[p.array for p in pieces], *extra)


def on_device(queries, keys, values, doc_lengths):
    rows = queries.shape[0]
    heads = keys.shape[1] // HEAD_DIM
    group = queries.shape[1] // keys.shape[1]
    count = lax.axis_size("seq")
    each = rows // DOC_UNIT
    longest = count * each // 2
    window = longest - 1 + each
    units = np.arange(count * each).reshape(count, each)
    if is_cube(count, each):
        low, high = (
            Piece(jnp.concatenate([keys[part], values[part]], axis=1), units[:, u : u + 1])
            for u, part in enumerate((slice(0, DOC_UNIT), slice(DOC_UNIT, rows)))
        )
        first, last = cube_exchange(low, high)
        return in_two(queries, doc_lengths, first, last, window, each, group, heads)
    out = None
    parts = PARTS_OF_HEADS
    for part in range(parts):
        first, last = heads * part // parts, heads * (part + 1) // parts
        columns = slice(first * HEAD_DIM, last * HEAD_DIM)
        both = jnp.concatenate([keys[:, columns], values[:, columns]], axis=1)
        pieces = gather_exchange(Piece(both, units))
        out = attend(
            queries, doc_lengths, pieces, window, each, group, first, last - first, out
        )
    return out


def is_cube(count, each):
    return (count, each) == (8, 2)


def solution(mesh):
    rows = P(("grp", "seq"), None)
    return jax.shard_map(
        on_device, mesh=mesh, in_specs=(rows, rows, rows, P("grp")), out_specs=rows, check_vma=False
    )
```

profile of v0, /device:TPU:12, one launch (start us, length us, event | category | flops | bytes accessed | tf_op | source)
XLA Modules:
  0.0 72.3 jit_solution(6364047890005293056)
XLA Ops:
  0.0 0.0 copy-start
  0.0 0.0 copy-start.1
  0.0 1.4 %fusion = (bf16[128,1024]{1,0:T(8,128)(2,1)S(1)}, bf16[128,1024]{1,0:T(8,128)(2,1)S(1)}, bf16[128,1024]{1,0:T(8,128)(2,1)S(1)}, bf16[128,1024]{1,0:T(8,128)(2,1)S(1)}) fusion(bf16[256,1024]{1,0:T(8,128)(2,1)} %param.5, bf16[256,1024]{1,0:T(8,128)(2,1)} %param.6), kind=kLoop, calls=%fused_computation.2 | loop fusion | bytes 2097152 | tf_op jit(solution)/shard_map/slice | solution.py:589
  1.5 0.7 collective-permute-start.2
  2.2 0.7 collective-permute-start.3
  2.9 1.3 %collective-permute-start.5 = (bf16[128,2048]{1,0:T(8,128)(2,1)S(1)}, bf16[128,2048]{1,0:T(8,128)(2,1)S(1)}, u32[]{:S(2)}, u32[]{:S(2)}) collective-permute-start(bf16[128,2048]{1,0:T(8,128)(2,1)S(1)} %pad_maximum_fusion.1.refs_1_), channel_id=1, source_target_pairs={{0,16},{4,20},{1,17},{5,21},{2,18},{6,22},{3,19},{7,23}} | collective-permute-start | bytes 1572872 | tf_op jit(solution)/shard_map/ppermute | solution.py:30
  4.2 1.3 %collective-permute-start.4 = (bf16[128,2048]{1,0:T(8,128)(2,1)S(1)}, bf16[128,2048]{1,0:T(8,128)(2,1)S(1)}, u32[]{:S(2)}, u32[]{:S(2)}) collective-permute-start(bf16[128,2048]{1,0:T(8,128)(2,1)S(1)} %pad_maximum_fusion.refs_0_), channel_id=1, source_target_pairs={{4,16},{8,20},{5,17},{9,21},{6,18},{10,22},{7,19},{11,23}} | collective-permute-start | bytes 1572872 | tf_op jit(solution)/shard_map/ppermute | solution.py:30
  5.5 3.4 %collective-permute-start.6 = (bf16[128,2048]{1,0:T(8,128)(2,1)S(1)}, bf16[128,2048]{1,0:T(8,128)(2,1)S(1)}, u32[]{:S(2)}, u32[]{:S(2)}) collective-permute-start(bf16[128,2048]{1,0:T(8,128)(2,1)S(1)} %pad_maximum_fusion.refs_0_), channel_id=1, source_target_pairs={{0,8},{4,12},{16,24},{20,28},{1,9},{5,13},{17,25},{21,29},{2,10},{... | collective-permute-start | bytes 1572872 | tf_op jit(solution)/shard_map/ppermute | solution.py:30
  8.9 0.0 collective-permute-done.2.refs_4_
  9.0 1.3 %collective-permute-start.1 = (bf16[128,2048]{1,0:T(8,128)(2,1)S(1)}, bf16[128,2048]{1,0:T(8,128)(2,1)S(1)}, u32[]{:S(2)}, u32[]{:S(2)}) collective-permute-start(bf16[128,2048]{1,0:T(8,128)(2,1)S(1)} %pad_maximum_fusion.1.refs_1_), channel_id=1, source_target_pairs={{0,4},{8,12},{16,20},{24,28},{1,5},{9,13},{17,21},{25,29},{2,6},{1... | collective-permute-start | bytes 1572872 | tf_op jit(solution)/shard_map/ppermute | solution.py:30
  10.3 0.0 collective-permute-done.3.refs_5_
  10.3 1.3 %collective-permute-start = (bf16[128,2048]{1,0:T(8,128)(2,1)S(1)}, bf16[128,2048]{1,0:T(8,128)(2,1)S(1)}, u32[]{:S(2)}, u32[]{:S(2)}) collective-permute-start(bf16[128,2048]{1,0:T(8,128)(2,1)S(1)} %pad_maximum_fusion.refs_0_), channel_id=1, source_target_pairs={{0,4},{8,12},{16,20},{24,28},{1,5},{9,13},{17,21},{25,29},{2,6},{1... | collective-permute-start | bytes 1572872 | tf_op jit(solution)/shard_map/ppermute | solution.py:30
  11.6 13.6 %collective-permute-done.5.refs_7_ = bf16[128,2048]{1,0:T(8,128)(2,1)S(1)} collective-permute-done((bf16[128,2048]{1,0:T(8,128)(2,1)S(1)}, bf16[128,2048]{1,0:T(8,128)(2,1)S(1)}, u32[]{:S(2)}, u32[]{:S(2)}) %collective-permute-start.5) | collective-permute-done | bytes 524320 | tf_op jit(solution)/shard_map/ppermute | solution.py:30
  25.2 3.2 %collective-permute-start.13 = (bf16[128,2048]{1,0:T(8,128)(2,1)S(1)}, bf16[128,2048]{1,0:T(8,128)(2,1)S(1)}, u32[]{:S(2)}, u32[]{:S(2)}) collective-permute-start(bf16[128,2048]{1,0:T(8,128)(2,1)S(1)} %pad_maximum_fusion.1.refs_1_), channel_id=1, source_target_pairs={{0,8},{4,12},{16,24},{20,28},{1,9},{5,13},{17,25},{21,29},{2,10},{... | collective-permute-start | bytes 1572872 | tf_op jit(solution)/shard_map/ppermute | solution.py:30
  28.4 1.3 %collective-permute-done.4.refs_6_ = bf16[128,2048]{1,0:T(8,128)(2,1)S(1)} collective-permute-done((bf16[128,2048]{1,0:T(8,128)(2,1)S(1)}, bf16[128,2048]{1,0:T(8,128)(2,1)S(1)}, u32[]{:S(2)}, u32[]{:S(2)}) %collective-permute-start.4) | collective-permute-done | bytes 524320 | tf_op jit(solution)/shard_map/ppermute | solution.py:30
  29.7 1.3 %collective-permute-start.7 = (bf16[128,2048]{1,0:T(8,128)(2,1)S(1)}, bf16[128,2048]{1,0:T(8,128)(2,1)S(1)}, u32[]{:S(2)}, u32[]{:S(2)}) collective-permute-start(bf16[128,2048]{1,0:T(8,128)(2,1)S(1)} %collective-permute-done.2.refs_4_), channel_id=1, source_target_pairs={{24,16},{25,17},{26,18},{27,19}} | collective-permute-start | bytes 1572872 | tf_op jit(solution)/shard_map/ppermute | solution.py:30
  31.0 0.0 collective-permute-done.6.refs_8_
  31.0 0.7 collective-permute-start.12
  31.7 0.0 collective-permute-done.1.refs_3_
  31.7 1.3 %collective-permute-start.11 = (bf16[128,2048]{1,0:T(8,128)(2,1)S(1)}, bf16[128,2048]{1,0:T(8,128)(2,1)S(1)}, u32[]{:S(2)}, u32[]{:S(2)}) collective-permute-start(bf16[128,2048]{1,0:T(8,128)(2,1)S(1)} %collective-permute-done.5.refs_7_), channel_id=1, source_target_pairs={{20,16},{21,17},{22,18},{23,19}} | collective-permute-start | bytes 1572872 | tf_op jit(solution)/shard_map/ppermute | solution.py:30
  33.0 0.0 collective-permute-done.refs_2_
  33.0 1.3 %collective-permute-start.14 = (bf16[128,2048]{1,0:T(8,128)(2,1)S(1)}, bf16[128,2048]{1,0:T(8,128)(2,1)S(1)}, u32[]{:S(2)}, u32[]{:S(2)}) collective-permute-start(bf16[128,2048]{1,0:T(8,128)(2,1)S(1)} %collective-permute-done.3.refs_5_), channel_id=1, source_target_pairs={{24,16},{28,20},{25,17},{29,21},{26,18},{30,22},{27,19},{31,23}} | collective-permute-start | bytes 1572872 | tf_op jit(solution)/shard_map/ppermute | solution.py:30
  34.3 4.7 %collective-permute-done.13.refs_0_ = bf16[128,2048]{1,0:T(8,128)(2,1)S(1)} collective-permute-done((bf16[128,2048]{1,0:T(8,128)(2,1)S(1)}, bf16[128,2048]{1,0:T(8,128)(2,1)S(1)}, u32[]{:S(2)}, u32[]{:S(2)}) %collective-permute-start.13) | collective-permute-done | bytes 524320 | tf_op jit(solution)/shard_map/ppermute | solution.py:30
  39.0 1.3 %collective-permute-start.10 = (bf16[128,2048]{1,0:T(8,128)(2,1)S(1)}, bf16[128,2048]{1,0:T(8,128)(2,1)S(1)}, u32[]{:S(2)}, u32[]{:S(2)}) collective-permute-start(bf16[128,2048]{1,0:T(8,128)(2,1)S(1)} %collective-permute-done.4.refs_6_), channel_id=1, source_target_pairs={{20,16},{21,17},{22,18},{23,19}} | collective-permute-start | bytes 1572872 | tf_op jit(solution)/shard_map/ppermute | solution.py:30
  40.3 2.2 %collective-permute-done.7.refs_9_ = bf16[128,2048]{1,0:T(8,128)(2,1)S(1)} collective-permute-done((bf16[128,2048]{1,0:T(8,128)(2,1)S(1)}, bf16[128,2048]{1,0:T(8,128)(2,1)S(1)}, u32[]{:S(2)}, u32[]{:S(2)}) %collective-permute-start.7) | collective-permute-done | bytes 524320 | tf_op jit(solution)/shard_map/ppermute | solution.py:30
  42.6 0.7 collective-permute-start.8
  43.2 0.0 collective-permute-done.12.refs_14_
  43.3 1.3 %collective-permute-start.9 = (bf16[128,2048]{1,0:T(8,128)(2,1)S(1)}, bf16[128,2048]{1,0:T(8,128)(2,1)S(1)}, u32[]{:S(2)}, u32[]{:S(2)}) collective-permute-start(bf16[128,2048]{1,0:T(8,128)(2,1)S(1)} %collective-permute-done.7.refs_9_), channel_id=1, source_target_pairs={{16,20},{17,21},{18,22},{19,23}} | collective-permute-start | bytes 1572872 | tf_op jit(solution)/shard_map/ppermute | solution.py:30
  44.6 0.0 collective-permute-done.11.refs_13_
  44.6 0.7 collective-permute-start.15
  45.3 6.7 %collective-permute-done.14.refs_1_ = bf16[128,2048]{1,0:T(8,128)(2,1)S(1)} collective-permute-done((bf16[128,2048]{1,0:T(8,128)(2,1)S(1)}, bf16[128,2048]{1,0:T(8,128)(2,1)S(1)}, u32[]{:S(2)}, u32[]{:S(2)}) %collective-permute-start.14) | collective-permute-done | bytes 524320 | tf_op jit(solution)/shard_map/ppermute | solution.py:30
  52.0 1.9 %collective-permute-start.16 = (bf16[128,2048]{1,0:T(8,128)(2,1)S(1)}, bf16[128,2048]{1,0:T(8,128)(2,1)S(1)}, u32[]{:S(2)}, u32[]{:S(2)}) collective-permute-start(bf16[128,2048]{1,0:T(8,128)(2,1)S(1)} %collective-permute-done.14.refs_1_), channel_id=1, source_target_pairs={{16,20},{20,16},{17,21},{21,17},{18,22},{22,18},{19,23},{23,19}} | collective-permute-start | bytes 1572872 | tf_op jit(solution)/shard_map/ppermute | solution.py:30
  53.9 0.0 collective-permute-done.10.refs_12_
  53.9 0.0 collective-permute-done.8.refs_10_
  53.9 0.0 collective-permute-done.9.refs_11_
  53.9 0.0 copy-done
  54.0 0.0 copy-done.1
  54.0 11.0 %shard_map.46 = (f32[8,2,512,256]{3,2,1,0:T(8,128)S(1)}, f32[8,2,512,128]{3,2,1,0:T(8,128)S(1)}) custom-call(s32[6]{0:T(128)S(1)} %copy-done.1, bf16[256,4096]{1,0:T(8,128)(2,1)S(1)} %copy-done, bf16[128,2048]{1,0:T(8,128)(2,1)S(1)} %pad_maximum_fusion.refs_0_, bf16[128,2048]{1,0:T(8,128)(2,1)S(1)} %pad_maximum_fusion.1.refs_1_, ...), custom_call_target="tpu_custom_call" | custom-call | flops 1879048192 | bytes 8388608 | tf_op jit(solution)/shard_map/pallas_call | solution.py:355
  65.0 0.0 collective-permute-done.15.refs_2_
  65.0 0.0 collective-permute-done.16.refs_3_
  65.0 7.3 %shard_map.47 = bf16[256,4096]{1,0:T(8,128)(2,1)} custom-call(s32[6]{0:T(128)S(1)} %copy-done.1, bf16[256,4096]{1,0:T(8,128)(2,1)S(1)} %copy-done, f32[8,2,512,256]{3,2,1,0:T(8,128)S(1)} %get-tuple-element.7.mixed_ref, f32[8,2,512,128]{3,2,1,0:T(8,128)S(1)} %get-tuple-element.8.top_ref, bf16[128,2048]{1,0:T(8,128)(2,1)S(1)} %collective-permute-done.13.refs_0_, ...), custom_call_target="tpu_custom_call" | custom-call | flops 536870912 | bytes 8388608 | tf_op jit(solution)/shard_map/pallas_call | solution.py:355
  (2 shorter events, 0.1 us)
Async XLA Ops:
  0.0 53.9 %copy-start = (bf16[256,4096]{1,0:T(8,128)(2,1)S(1)}, bf16[256,4096]{1,0:T(8,128)(2,1)}, u32[]{:S(2)}) copy-start(bf16[256,4096]{1,0:T(8,128)(2,1)} %q_hbm.3) | copy-start | bytes 6291460
  0.0 54.0 %copy-start.1 = (s32[6]{0:T(128)S(1)}, s32[6]{0:T(128)}, u32[]{:S(2)}) copy-start(s32[6]{0:T(128)} %docs_ref.3) | copy-start | bytes 76
  1.5 7.5 %collective-permute-start.2 = (bf16[128,2048]{1,0:T(8,128)(2,1)S(1)}, bf16[128,2048]{1,0:T(8,128)(2,1)S(1)}, u32[]{:S(2)}, u32[]{:S(2)}) collective-permute-start(bf16[128,2048]{1,0:T(8,128)(2,1)S(1)} %pad_maximum_fusion.refs_0_), channel_id=1, source_target_pairs={{12,24},{13,25},{14,26},{15,27}} | collective-permute-start | bytes 1572872 | tf_op jit(solution)/shard_map/ppermute | solution.py:30
  2.2 8.1 %collective-permute-start.3 = (bf16[128,2048]{1,0:T(8,128)(2,1)S(1)}, bf16[128,2048]{1,0:T(8,128)(2,1)S(1)}, u32[]{:S(2)}, u32[]{:S(2)}) collective-permute-start(bf16[128,2048]{1,0:T(8,128)(2,1)S(1)} %pad_maximum_fusion.1.refs_1_), channel_id=1, source_target_pairs={{8,24},{12,28},{9,25},{13,29},{10,26},{14,30},{11,27},{15,31}} | collective-permute-start | bytes 1572872 | tf_op jit(solution)/shard_map/ppermute | solution.py:30
  2.9 22.3 %collective-permute-start.5 = (bf16[128,2048]{1,0:T(8,128)(2,1)S(1)}, bf16[128,2048]{1,0:T(8,128)(2,1)S(1)}, u32[]{:S(2)}, u32[]{:S(2)}) collective-permute-start(bf16[128,2048]{1,0:T(8,128)(2,1)S(1)} %pad_maximum_fusion.1.refs_1_), channel_id=1, source_target_pairs={{0,16},{4,20},{1,17},{5,21},{2,18},{6,22},{3,19},{7,23}} | collective-permute-start | bytes 1572872 | tf_op jit(solution)/shard_map/ppermute | solution.py:30
  4.2 25.5 %collective-permute-start.4 = (bf16[128,2048]{1,0:T(8,128)(2,1)S(1)}, bf16[128,2048]{1,0:T(8,128)(2,1)S(1)}, u32[]{:S(2)}, u32[]{:S(2)}) collective-permute-start(bf16[128,2048]{1,0:T(8,128)(2,1)S(1)} %pad_maximum_fusion.refs_0_), channel_id=1, source_target_pairs={{4,16},{8,20},{5,17},{9,21},{6,18},{10,22},{7,19},{11,23}} | collective-permute-start | bytes 1572872 | tf_op jit(solution)/shard_map/ppermute | solution.py:30
  5.5 25.5 %collective-permute-start.6 = (bf16[128,2048]{1,0:T(8,128)(2,1)S(1)}, bf16[128,2048]{1,0:T(8,128)(2,1)S(1)}, u32[]{:S(2)}, u32[]{:S(2)}) collective-permute-start(bf16[128,2048]{1,0:T(8,128)(2,1)S(1)} %pad_maximum_fusion.refs_0_), channel_id=1, source_target_pairs={{0,8},{4,12},{16,24},{20,28},{1,9},{5,13},{17,25},{21,29},{2,10},{... | collective-permute-start | bytes 1572872 | tf_op jit(solution)/shard_map/ppermute | solution.py:30
  9.0 22.8 %collective-permute-start.1 = (bf16[128,2048]{1,0:T(8,128)(2,1)S(1)}, bf16[128,2048]{1,0:T(8,128)(2,1)S(1)}, u32[]{:S(2)}, u32[]{:S(2)}) collective-permute-start(bf16[128,2048]{1,0:T(8,128)(2,1)S(1)} %pad_maximum_fusion.1.refs_1_), channel_id=1, source_target_pairs={{0,4},{8,12},{16,20},{24,28},{1,5},{9,13},{17,21},{25,29},{2,6},{1... | collective-permute-start | bytes 1572872 | tf_op jit(solution)/shard_map/ppermute | solution.py:30
  10.3 22.7 %collective-permute-start = (bf16[128,2048]{1,0:T(8,128)(2,1)S(1)}, bf16[128,2048]{1,0:T(8,128)(2,1)S(1)}, u32[]{:S(2)}, u32[]{:S(2)}) collective-permute-start(bf16[128,2048]{1,0:T(8,128)(2,1)S(1)} %pad_maximum_fusion.refs_0_), channel_id=1, source_target_pairs={{0,4},{8,12},{16,20},{24,28},{1,5},{9,13},{17,21},{25,29},{2,6},{1... | collective-permute-start | bytes 1572872 | tf_op jit(solution)/shard_map/ppermute | solution.py:30
  25.2 13.8 %collective-permute-start.13 = (bf16[128,2048]{1,0:T(8,128)(2,1)S(1)}, bf16[128,2048]{1,0:T(8,128)(2,1)S(1)}, u32[]{:S(2)}, u32[]{:S(2)}) collective-permute-start(bf16[128,2048]{1,0:T(8,128)(2,1)S(1)} %pad_maximum_fusion.1.refs_1_), channel_id=1, source_target_pairs={{0,8},{4,12},{16,24},{20,28},{1,9},{5,13},{17,25},{21,29},{2,10},{... | collective-permute-start | bytes 1572872 | tf_op jit(solution)/shard_map/ppermute | solution.py:30
  29.7 12.9 %collective-permute-start.7 = (bf16[128,2048]{1,0:T(8,128)(2,1)S(1)}, bf16[128,2048]{1,0:T(8,128)(2,1)S(1)}, u32[]{:S(2)}, u32[]{:S(2)}) collective-permute-start(bf16[128,2048]{1,0:T(8,128)(2,1)S(1)} %collective-permute-done.2.refs_4_), channel_id=1, source_target_pairs={{24,16},{25,17},{26,18},{27,19}} | collective-permute-start | bytes 1572872 | tf_op jit(solution)/shard_map/ppermute | solution.py:30
  31.0 12.2 %collective-permute-start.12 = (bf16[128,2048]{1,0:T(8,128)(2,1)S(1)}, bf16[128,2048]{1,0:T(8,128)(2,1)S(1)}, u32[]{:S(2)}, u32[]{:S(2)}) collective-permute-start(bf16[128,2048]{1,0:T(8,128)(2,1)S(1)} %collective-permute-done.3.refs_5_), channel_id=1, source_target_pairs={{28,24},{29,25},{30,26},{31,27}} | collective-permute-start | bytes 1572872 | tf_op jit(solution)/shard_map/ppermute | solution.py:30
  31.7 12.9 %collective-permute-start.11 = (bf16[128,2048]{1,0:T(8,128)(2,1)S(1)}, bf16[128,2048]{1,0:T(8,128)(2,1)S(1)}, u32[]{:S(2)}, u32[]{:S(2)}) collective-permute-start(bf16[128,2048]{1,0:T(8,128)(2,1)S(1)} %collective-permute-done.5.refs_7_), channel_id=1, source_target_pairs={{20,16},{21,17},{22,18},{23,19}} | collective-permute-start | bytes 1572872 | tf_op jit(solution)/shard_map/ppermute | solution.py:30
  33.0 19.0 %collective-permute-start.14 = (bf16[128,2048]{1,0:T(8,128)(2,1)S(1)}, bf16[128,2048]{1,0:T(8,128)(2,1)S(1)}, u32[]{:S(2)}, u32[]{:S(2)}) collective-permute-start(bf16[128,2048]{1,0:T(8,128)(2,1)S(1)} %collective-permute-done.3.refs_5_), channel_id=1, source_target_pairs={{24,16},{28,20},{25,17},{29,21},{26,18},{30,22},{27,19},{31,23}} | collective-permute-start | bytes 1572872 | tf_op jit(solution)/shard_map/ppermute | solution.py:30
  39.0 14.9 %collective-permute-start.10 = (bf16[128,2048]{1,0:T(8,128)(2,1)S(1)}, bf16[128,2048]{1,0:T(8,128)(2,1)S(1)}, u32[]{:S(2)}, u32[]{:S(2)}) collective-permute-start(bf16[128,2048]{1,0:T(8,128)(2,1)S(1)} %collective-permute-done.4.refs_6_), channel_id=1, source_target_pairs={{20,16},{21,17},{22,18},{23,19}} | collective-permute-start | bytes 1572872 | tf_op jit(solution)/shard_map/ppermute | solution.py:30
  42.6 11.4 %collective-permute-start.8 = (bf16[128,2048]{1,0:T(8,128)(2,1)S(1)}, bf16[128,2048]{1,0:T(8,128)(2,1)S(1)}, u32[]{:S(2)}, u32[]{:S(2)}) collective-permute-start(bf16[128,2048]{1,0:T(8,128)(2,1)S(1)} %collective-permute-done.6.refs_8_), channel_id=1, source_target_pairs={{8,12},{12,8},{24,28},{28,24},{9,13},{13,9},{25,29},{29,25},{10,14... | collective-permute-start | bytes 1572872 | tf_op jit(solution)/shard_map/ppermute | solution.py:30
  43.3 10.7 %collective-permute-start.9 = (bf16[128,2048]{1,0:T(8,128)(2,1)S(1)}, bf16[128,2048]{1,0:T(8,128)(2,1)S(1)}, u32[]{:S(2)}, u32[]{:S(2)}) collective-permute-start(bf16[128,2048]{1,0:T(8,128)(2,1)S(1)} %collective-permute-done.7.refs_9_), channel_id=1, source_target_pairs={{16,20},{17,21},{18,22},{19,23}} | collective-permute-start | bytes 1572872 | tf_op jit(solution)/shard_map/ppermute | solution.py:30
  44.6 20.4 %collective-permute-start.15 = (bf16[128,2048]{1,0:T(8,128)(2,1)S(1)}, bf16[128,2048]{1,0:T(8,128)(2,1)S(1)}, u32[]{:S(2)}, u32[]{:S(2)}) collective-permute-start(bf16[128,2048]{1,0:T(8,128)(2,1)S(1)} %collective-permute-done.13.refs_0_), channel_id=1, source_target_pairs={{8,12},{12,8},{24,28},{28,24},{9,13},{13,9},{25,29},{29,25},{10,14... | collective-permute-start | bytes 1572872 | tf_op jit(solution)/shard_map/ppermute | solution.py:30
  52.0 13.0 %collective-permute-start.16 = (bf16[128,2048]{1,0:T(8,128)(2,1)S(1)}, bf16[128,2048]{1,0:T(8,128)(2,1)S(1)}, u32[]{:S(2)}, u32[]{:S(2)}) collective-permute-start(bf16[128,2048]{1,0:T(8,128)(2,1)S(1)} %collective-permute-done.14.refs_1_), channel_id=1, source_target_pairs={{16,20},{20,16},{17,21},{21,17},{18,22},{22,18},{19,23},{23,19}} | collective-permute-start | bytes 1572872 | tf_op jit(solution)/shard_map/ppermute | solution.py:30
where the time goes:
time: 72.6 us; the launch traced here: 72.3 us
  waiting for transfers between devices  28.6 us (39%)
  starting transfers between devices  23.7 us (33%)
  Pallas kernels  18.3 us (25%)
  local copies, waits for them, and re-layouts  1.41 us (2%)
    ppermute x17, waiting for transfers between devices, to(): return Piece(lax.ppermute(self.array, 'seq', pairs), units)  28.6 us
    ppermute x17, starting transfers between devices, to(): return Piece(lax.ppermute(self.array, 'seq', pairs), units)  23.7 us
    pallas_call x2, Pallas kernels, call(): pl.pallas_call(functools.partial(kernel, plan), out_shape=shapes, grid_sp...  18.3 us
  transfers between devices with their start and end apart: 17, of which 5 were waited for; matrix products, arithmetic and copies ran while one was open for 0% of the time, Pallas kernels for 15%

commit v1 on v0

--- a/solution.py
+++ b/solution.py
@@ -36,11 +36,12 @@
     swap = lambda *chips: [(chip(c, b), chip(c, 1 - b)) for c in chips for b in both]
     next_chip = [(chip(c, b), chip(c + 1, b)) for c in (0, 2) for b in both]
     beside = [(chip(c, 0), chip(c, 1)) for c in range(4)]
+    b_low = low.to([(chip(0, 1), chip(2, 0))])
+    b_high = high.to([(chip(0, b), chip(2, b)) for b in both])
+    near_low = low.to([*next_chip, (chip(1, 0), chip(2, 1))])
+    near_high = high.to(next_chip)
     a_low = low.to([(chip(1, 1), chip(3, 0))])
     a_high = high.to([(chip(1, b), chip(3, b)) for b in both])
-    b_low = low.to([(chip(0, 1), chip(2, 0)), (chip(1, 0), chip(2, 1))])
-    b_high = high.to([(chip(0, b), chip(2, b)) for b in both])
-    near_low, near_high = low.to(next_chip), high.to(next_chip)
     on_low = a_low.to([(chip(3, 0), chip(2, 0))])
     on_high = a_high.to([(chip(3, b), chip(2, b)) for b in both])
     first = [
@@ -54,9 +55,8 @@
         b_high,
         near_low,
         on_low,
-        near_low.to(swap(1, 3)),
+        near_low.to([*swap(1, 3), (chip(2, 1), chip(2, 0))]),
         on_low.to([(chip(2, 0), chip(2, 1))]),
-        b_low.to([(chip(2, 1), chip(2, 0))]),
         b_high.to([(chip(2, 1), chip(2, 0))]),
         a_high.to([(chip(3, 1), chip(3, 0))]),
     ]
@@ -166,25 +166,26 @@
 
 
 CHUNK = 2
-AT_ONCE = 2
+FIRST_HEADS, LAST_HEADS = 4, 8
 
 
 def unit_copies(pieces, slots, table, sems, buf, device, lowest, place):
-    def each_copy(act):
-        for t, (number, block) in enumerate(slots):
-            unit = held_unit(table[:, t], device)
-
-            @pl.when(unit >= lowest)
-            def _():
-                act(
-                    pltpu.make_async_copy(
-                        pieces[number].at[pl.ds(block * DOC_UNIT, DOC_UNIT)],
-                        buf.at[rows_of(place(unit), 1)],
-                        sems.at[t],
-                    )
-                )
-
-    return each_copy
+    jobs = []
+    for t, (number, block) in enumerate(slots):
+        unit = held_unit(table[:, t], device)
+        copy = pltpu.make_async_copy(
+            pieces[number].at[pl.ds(block * DOC_UNIT, DOC_UNIT)],
+            buf.at[rows_of(place(unit), 1)],
+            sems.at[t],
+        )
+        jobs.append((unit >= lowest, copy))
+        pl.when(unit >= lowest)(copy.start)
+
+    def arrived():
+        for wanted, copy in jobs:
+            pl.when(wanted)(copy.wait)
+
+    return arrived
 
 
 def late_units(device):
@@ -192,10 +193,10 @@
     return 4 * chip - 3, 4 * chip - 1
 
 
-def first_kernel(plan, docs_ref, q_hbm, *refs):
+def first_kernel(plan, docs_ref, q_all, *refs):
     slots, table, n_pieces, window, each, group, heads = plan
     pieces = refs[:n_pieces]
-    mixed_ref, top_ref, q_all, buf, sems, q_sem = refs[n_pieces:]
+    mixed_ref, top_ref, buf, sems = refs[n_pieces:]
     device = lax.axis_index("seq")
     first_unit = device * each
     base = first_unit + each - window
@@ -205,17 +206,13 @@
     def place(unit):
         return unit - base - (unit > late[0]).astype(jnp.int32) - (unit > late[1]).astype(jnp.int32)
 
-    each_copy = unit_copies(
+    unit_copies(
         pieces, slots, table, sems, buf, device, doc_start(docs_ref, first_unit), place
-    )
-    q_copy = pltpu.make_async_copy(q_hbm, q_all, q_sem)
-    each_copy(lambda copy: copy.start())
-    q_copy.start()
-    each_copy(lambda copy: copy.wait())
-    q_copy.wait()
+    )()
+    steps = heads // FIRST_HEADS * each
 
     def one_step(step, carry):
-        pair, part = lax.div(step, each), lax.rem(step, each)
+        first_head, part = lax.div(step, each) * FIRST_HEADS, lax.rem(step, each)
         unit = first_unit + part
         start = doc_start(docs_ref, unit)
         skipped = sum(((u >= start) & (u <= unit)).astype(jnp.int32) for u in late)
@@ -225,70 +222,63 @@
             @pl.when(here == units)
             def _():
                 rows = rows_of(place(unit) - units + 1, units)
-                jobs = [(h, g) for h in range(AT_ONCE) for g in range(0, group, CHUNK)]
+                jobs = [(h, g) for h in range(FIRST_HEADS) for g in range(0, group, CHUNK)]
 
                 def begin(job):
-                    head, g = pair * AT_ONCE + job[0], job[1]
+                    head, g = first_head + job[0], job[1]
                     q = q_all[rows_of(part, 1), columns_of(head, columns)]
                     keys = buf[rows, columns_of(head)]
                     return scores_of(stacked(q, range(g, g + CHUNK)), keys)
 
                 def end(job, scores):
                     h, g = job
-                    head = pair * AT_ONCE + h
+                    head = first_head + h
                     scores = masked_last(scores, units)
                     top = jnp.max(scores, axis=1, keepdims=True)
                     weights = jnp.exp2((scores - top) * FACTOR)
                     mine = pl.ds(g * DOC_UNIT, CHUNK * DOC_UNIT)
-                    mixed_ref[step, h, mine] = mixed(weights, buf[rows, columns_of(heads + head)])
-                    top_ref[step, h, mine] = jnp.broadcast_to(top, (CHUNK * DOC_UNIT, HEAD_DIM))
+                    mixed_ref[head, part, mine] = mixed(weights, buf[rows, columns_of(heads + head)])
+                    top_ref[head, part, mine] = jnp.broadcast_to(top, (CHUNK * DOC_UNIT, HEAD_DIM))
 
                 in_turn(jobs, begin, end)
 
         return carry
 
-    lax.fori_loop(0, heads // AT_ONCE * each, one_step, 0)
-
-
-def last_kernel(plan, docs_ref, q_hbm, mixed_ref, top_ref, *refs):
+    lax.fori_loop(0, steps, one_step, 0)
+
+
+def last_kernel(plan, docs_ref, q_all, mixed_ref, top_ref, *refs):
     slots, table, n_pieces, _, each, group, heads = plan
     pieces = refs[:n_pieces]
-    out_hbm, q_all, buf, out_all, sems, q_sem, out_sems = refs[n_pieces:]
+    out_hbm, buf, out_all, sems, out_sems = refs[n_pieces:]
     device = lax.axis_index("seq")
     first_unit = device * each
     late = late_units(device)
     columns = group * HEAD_DIM
-    steps = heads // AT_ONCE * each
-
+    steps = heads // LAST_HEADS * each
     place = lambda unit: (unit > late[0]).astype(jnp.int32)
-    each_copy = unit_copies(pieces, slots, table, sems, buf, device, 0, place)
-    q_copy = pltpu.make_async_copy(q_hbm, q_all, q_sem)
-
-    def copy_out(pair):
-        there = columns_of(pair, AT_ONCE * columns)
-        return pltpu.make_async_copy(out_all.at[:, there], out_hbm.at[:, there], out_sems.at[pair])
-
-    each_copy(lambda copy: copy.start())
-    q_copy.start()
-    each_copy(lambda copy: copy.wait())
-    q_copy.wait()
+    unit_copies(pieces, slots, table, sems, buf, device, 0, place)()
+
+    def copy_out(part):
+        there = rows_of(part, 1)
+        return pltpu.make_async_copy(out_all.at[there], out_hbm.at[there], out_sems.at[part])
 
     def one_step(step, carry):
-        pair, part = lax.div(step, each), lax.rem(step, each)
+        part, first_head = lax.rem(step, each), lax.div(step, each) * LAST_HEADS
         unit = first_unit + part
         start = doc_start(docs_ref, unit)
         count = sum((u >= start).astype(jnp.int32) for u in late)
-        jobs = [(h, g) for h in range(AT_ONCE) for g in range(0, group, CHUNK)]
+        jobs = [(h, g) for h in range(LAST_HEADS) for g in range(0, group, CHUNK)]
 
         def older(ref, job):
-            return ref[step, job[0], pl.ds(job[1] * DOC_UNIT, CHUNK * DOC_UNIT)]
+            return ref[first_head + job[0], part, pl.ds(job[1] * DOC_UNIT, CHUNK * DOC_UNIT)]
 
         def mean(result):
             return result[:, :HEAD_DIM] / result[:, HEAD_DIM:]
 
         def store(job, rows):
             for k in range(CHUNK):
-                head = (pair * AT_ONCE + job[0]) * group + job[1] + k
+                head = (first_head + job[0]) * group + job[1] + k
                 out_all[rows_of(part, 1), columns_of(head)] = rows[
                     k * DOC_UNIT : (k + 1) * DOC_UNIT
                 ].astype(out_all.dtype)
@@ -301,12 +291,12 @@
         @pl.when(count > 0)
         def _():
             def begin(job):
-                head = pair * AT_ONCE + job[0]
+                head = first_head + job[0]
                 q = q_all[rows_of(part, 1), columns_of(head, columns)]
                 return scores_of(stacked(q, range(job[1], job[1] + CHUNK)), buf[:, columns_of(head)])
 
             def end(job, scores):
-                head = pair * AT_ONCE + job[0]
+                head = first_head + job[0]
                 column = lax.broadcasted_iota(jnp.int32, scores.shape, 1)
                 scores = jnp.where(column >= (2 - count) * DOC_UNIT, scores, -jnp.inf)
                 old = older(top_ref, job)
@@ -318,24 +308,23 @@
 
             in_turn(jobs, begin, end)
 
-        @pl.when(part == each - 1)
+        @pl.when(first_head == heads - LAST_HEADS)
         def _():
-            copy_out(pair).start()
+            copy_out(part).start()
 
         return carry
 
     lax.fori_loop(0, steps, one_step, 0)
-    for pair in range(heads // AT_ONCE):
-        copy_out(pair).wait()
+    for part in range(each):
+        copy_out(part).wait()
 
 
 def in_two(queries, doc_lengths, first, last, window, each, group, heads):
     rows = each * DOC_UNIT
     dtype = queries.dtype
-    steps = heads // AT_ONCE * each
     anywhere = pl.BlockSpec(memory_space=pl.ANY)
     dma = pltpu.SemaphoreType.DMA
-    tile = (steps, AT_ONCE, group * DOC_UNIT, HEAD_DIM)
+    tile = (heads, each, group * DOC_UNIT, HEAD_DIM)
     state = (
         pltpu.VMEM((*tile[:-1], 2 * HEAD_DIM), jnp.float32),
         pltpu.VMEM(tile, jnp.float32),
@@ -347,7 +336,6 @@
         slots, table = slots_of(pieces, window, each, wanted)
         plan = (slots, table, len(pieces), window, each, group, heads)
         scratch = [
-            pltpu.VMEM(queries.shape, dtype),
             pltpu.VMEM((held_rows, 2 * heads * HEAD_DIM), dtype),
             *scratch(len(slots)),
         ]
@@ -374,10 +362,10 @@
         lambda device, unit: not is_late(device, unit),
         (window - 2) * DOC_UNIT,
         (queries,),
-        (anywhere,),
+        (on_chip,),
         state,
         (on_chip, on_chip),
-        lambda n: [dma((n,)), dma],
+        lambda n: [dma((n,))],
     )
     return call(
         last_kernel,
@@ -385,10 +373,10 @@
         is_late,
         2 * DOC_UNIT,
         (queries, *so_far),
-        (anywhere, on_chip, on_chip),
+        (on_chip, on_chip, on_chip),
         jax.ShapeDtypeStruct(queries.shape, dtype),
         anywhere,
-        lambda n: [pltpu.VMEM(queries.shape, dtype), dma((n,)), dma, dma((heads // AT_ONCE,))],
+        lambda n: [pltpu.VMEM(queries.shape, dtype), dma((n,)), dma((each,))],
     )
 
 
@@ -610,6 +598,4 @@
 
 def solution(mesh):
     rows = P(("grp", "seq"), None)
-    return jax.shard_map(
-        on_device, mesh=mesh, in_specs=(rows, rows, rows, P("grp")), out_specs=rows, check_vma=False
-    )
+    return jax.shard_map(on_device, mesh=mesh, in_specs=(rows, rows, rows, P("grp")), out_specs=rows, check_vma=False)

time: 72.6 us -> 66.8 us (0.920)
  Pallas kernels: 18.3 us -> 15.6 us
  waiting for transfers between devices: 28.6 us -> 26 us
    pallas_call x2, Pallas kernels: 18.3 us -> 15.6 us  [call(): pl.pallas_call(functools.partial(kernel, plan), out_shape=shapes, grid_sp...]
    ppermute x17 -> x16, waiting for transfers between devices: 28.6 us -> 26 us  [to(): return Piece(lax.ppermute(self.array, 'seq', pairs), units)]
    ppermute x17 -> x16, starting transfers between devices: 23.7 us -> 23.1 us  [to(): return Piece(lax.ppermute(self.array, 'seq', pairs), units)]
  transfers between devices with their start and end apart: 17 -> 16, of which waited for: 5 -> 4; matrix products, arithmetic and copies ran while one was open for 0% -> 0% of each run, Pallas kernels for 15% -> 14%
where the time goes in v1:
time: 66.8 us; the launch traced here: 66.5 us
  waiting for transfers between devices  26 us (39%)
  starting transfers between devices  23.1 us (35%)
  Pallas kernels  15.6 us (23%)
  local copies, waits for them, and re-layouts  1.41 us (2%)
    ppermute x16, waiting for transfers between devices, to(): return Piece(lax.ppermute(self.array, 'seq', pairs), units)  26 us
    ppermute x16, starting transfers between devices, to(): return Piece(lax.ppermute(self.array, 'seq', pairs), units)  23.1 us
    pallas_call x2, Pallas kernels, call(): pl.pallas_call(functools.partial(kernel, plan), out_shape=shapes, grid_sp...  15.6 us
    slice x1, local copies, waits for them, and re-layouts, on_device(): keys[part]  1.4 us
  transfers between devices with their start and end apart: 16, of which 4 were waited for; matrix products, arithmetic and copies ran while one was open for 0% of the time, Pallas kernels for 14%

profile of v1, /device:TPU:12, one launch (start us, length us, event | category | flops | bytes accessed | tf_op | source)
XLA Modules:
  0.0 66.5 jit_solution(8847306027493801853)
XLA Ops:
  0.0 0.0 copy-start
  0.0 0.0 copy-start.1
  0.0 1.4 %fusion = (bf16[128,1024]{1,0:T(8,128)(2,1)S(1)}, bf16[128,1024]{1,0:T(8,128)(2,1)S(1)}, bf16[128,1024]{1,0:T(8,128)(2,1)S(1)}, bf16[128,1024]{1,0:T(8,128)(2,1)S(1)}) fusion(bf16[256,1024]{1,0:T(8,128)(2,1)} %param.5, bf16[256,1024]{1,0:T(8,128)(2,1)} %param.6), kind=kLoop, calls=%fused_computation.2 | loop fusion | bytes 2097152 | tf_op jit(solution)/shard_map/slice | solution.py:577
  1.5 0.7 %collective-permute-start.2 = (bf16[128,2048]{1,0:T(8,128)(2,1)S(1)}, bf16[128,2048]{1,0:T(8,128)(2,1)S(1)}, u32[]{:S(2)}, u32[]{:S(2)}) collective-permute-start(bf16[128,2048]{1,0:T(8,128)(2,1)S(1)} %pad_maximum_fusion.refs_0_), channel_id=1, source_target_pairs={{12,24},{13,25},{14,26},{15,27}} | collective-permute-start | bytes 1572872 | tf_op jit(solution)/shard_map/ppermute | solution.py:30
  2.2 0.7 %collective-permute-start.3 = (bf16[128,2048]{1,0:T(8,128)(2,1)S(1)}, bf16[128,2048]{1,0:T(8,128)(2,1)S(1)}, u32[]{:S(2)}, u32[]{:S(2)}) collective-permute-start(bf16[128,2048]{1,0:T(8,128)(2,1)S(1)} %pad_maximum_fusion.1.refs_1_), channel_id=1, source_target_pairs={{8,24},{12,28},{9,25},{13,29},{10,26},{14,30},{11,27},{15,31}} | collective-permute-start | bytes 1572872 | tf_op jit(solution)/shard_map/ppermute | solution.py:30
  2.9 1.3 %collective-permute-start.5 = (bf16[128,2048]{1,0:T(8,128)(2,1)S(1)}, bf16[128,2048]{1,0:T(8,128)(2,1)S(1)}, u32[]{:S(2)}, u32[]{:S(2)}) collective-permute-start(bf16[128,2048]{1,0:T(8,128)(2,1)S(1)} %pad_maximum_fusion.1.refs_1_), channel_id=1, source_target_pairs={{0,16},{4,20},{1,17},{5,21},{2,18},{6,22},{3,19},{7,23}} | collective-permute-start | bytes 1572872 | tf_op jit(solution)/shard_map/ppermute | solution.py:30
  4.2 4.0 %collective-permute-start.6 = (bf16[128,2048]{1,0:T(8,128)(2,1)S(1)}, bf16[128,2048]{1,0:T(8,128)(2,1)S(1)}, u32[]{:S(2)}, u32[]{:S(2)}) collective-permute-start(bf16[128,2048]{1,0:T(8,128)(2,1)S(1)} %pad_maximum_fusion.refs_0_), channel_id=1, source_target_pairs={{0,8},{4,12},{16,24},{20,28},{8,20},{1,9},{5,13},{17,25},{21,29},{... | collective-permute-start | bytes 1572872 | tf_op jit(solution)/shard_map/ppermute | solution.py:30
  8.2 1.3 %collective-permute-start.1 = (bf16[128,2048]{1,0:T(8,128)(2,1)S(1)}, bf16[128,2048]{1,0:T(8,128)(2,1)S(1)}, u32[]{:S(2)}, u32[]{:S(2)}) collective-permute-start(bf16[128,2048]{1,0:T(8,128)(2,1)S(1)} %pad_maximum_fusion.1.refs_1_), channel_id=1, source_target_pairs={{0,4},{8,12},{16,20},{24,28},{1,5},{9,13},{17,21},{25,29},{2,6},{1... | collective-permute-start | bytes 1572872 | tf_op jit(solution)/shard_map/ppermute | solution.py:30
  9.6 0.0 collective-permute-done.2.refs_4_
  9.6 1.3 %collective-permute-start = (bf16[128,2048]{1,0:T(8,128)(2,1)S(1)}, bf16[128,2048]{1,0:T(8,128)(2,1)S(1)}, u32[]{:S(2)}, u32[]{:S(2)}) collective-permute-start(bf16[128,2048]{1,0:T(8,128)(2,1)S(1)} %pad_maximum_fusion.refs_0_), channel_id=1, source_target_pairs={{0,4},{8,12},{16,20},{24,28},{1,5},{9,13},{17,21},{25,29},{2,6},{1... | collective-permute-start | bytes 1572872 | tf_op jit(solution)/shard_map/ppermute | solution.py:30
  10.9 0.0 collective-permute-done.3.refs_5_
  10.9 1.3 %collective-permute-start.4 = (bf16[128,2048]{1,0:T(8,128)(2,1)S(1)}, bf16[128,2048]{1,0:T(8,128)(2,1)S(1)}, u32[]{:S(2)}, u32[]{:S(2)}) collective-permute-start(bf16[128,2048]{1,0:T(8,128)(2,1)S(1)} %pad_maximum_fusion.refs_0_), channel_id=1, source_target_pairs={{4,16},{5,17},{6,18},{7,19}} | collective-permute-start | bytes 1572872 | tf_op jit(solution)/shard_map/ppermute | solution.py:30
  12.2 13.0 %collective-permute-done.5.refs_7_ = bf16[128,2048]{1,0:T(8,128)(2,1)S(1)} collective-permute-done((bf16[128,2048]{1,0:T(8,128)(2,1)S(1)}, bf16[128,2048]{1,0:T(8,128)(2,1)S(1)}, u32[]{:S(2)}, u32[]{:S(2)}) %collective-permute-start.5) | collective-permute-done | bytes 524320 | tf_op jit(solution)/shard_map/ppermute | solution.py:30
  25.2 1.3 %collective-permute-start.12 = (bf16[128,2048]{1,0:T(8,128)(2,1)S(1)}, bf16[128,2048]{1,0:T(8,128)(2,1)S(1)}, u32[]{:S(2)}, u32[]{:S(2)}) collective-permute-start(bf16[128,2048]{1,0:T(8,128)(2,1)S(1)} %pad_maximum_fusion.1.refs_1_), channel_id=1, source_target_pairs={{0,8},{4,12},{16,24},{20,28},{1,9},{5,13},{17,25},{21,29},{2,10},{... | collective-permute-start | bytes 1572872 | tf_op jit(solution)/shard_map/ppermute | solution.py:30
  26.5 0.0 collective-permute-done.6.refs_8_
  26.5 1.3 %collective-permute-start.7 = (bf16[128,2048]{1,0:T(8,128)(2,1)S(1)}, bf16[128,2048]{1,0:T(8,128)(2,1)S(1)}, u32[]{:S(2)}, u32[]{:S(2)}) collective-permute-start(bf16[128,2048]{1,0:T(8,128)(2,1)S(1)} %collective-permute-done.2.refs_4_), channel_id=1, source_target_pairs={{24,16},{25,17},{26,18},{27,19}} | collective-permute-start | bytes 1572872 | tf_op jit(solution)/shard_map/ppermute | solution.py:30
  27.8 0.0 collective-permute-done.1.refs_3_
  27.9 0.7 %collective-permute-start.11 = (bf16[128,2048]{1,0:T(8,128)(2,1)S(1)}, bf16[128,2048]{1,0:T(8,128)(2,1)S(1)}, u32[]{:S(2)}, u32[]{:S(2)}) collective-permute-start(bf16[128,2048]{1,0:T(8,128)(2,1)S(1)} %collective-permute-done.3.refs_5_), channel_id=1, source_target_pairs={{28,24},{29,25},{30,26},{31,27}} | collective-permute-start | bytes 1572872 | tf_op jit(solution)/shard_map/ppermute | solution.py:30
  28.6 0.0 collective-permute-done.refs_2_
  28.6 1.3 %collective-permute-start.13 = (bf16[128,2048]{1,0:T(8,128)(2,1)S(1)}, bf16[128,2048]{1,0:T(8,128)(2,1)S(1)}, u32[]{:S(2)}, u32[]{:S(2)}) collective-permute-start(bf16[128,2048]{1,0:T(8,128)(2,1)S(1)} %collective-permute-done.3.refs_5_), channel_id=1, source_target_pairs={{24,16},{28,20},{25,17},{29,21},{26,18},{30,22},{27,19},{31,23}} | collective-permute-start | bytes 1572872 | tf_op jit(solution)/shard_map/ppermute | solution.py:30
  29.9 0.0 collective-permute-done.4.refs_6_
  29.9 1.3 %collective-permute-start.10 = (bf16[128,2048]{1,0:T(8,128)(2,1)S(1)}, bf16[128,2048]{1,0:T(8,128)(2,1)S(1)}, u32[]{:S(2)}, u32[]{:S(2)}) collective-permute-start(bf16[128,2048]{1,0:T(8,128)(2,1)S(1)} %collective-permute-done.5.refs_7_), channel_id=1, source_target_pairs={{20,16},{21,17},{22,18},{23,19}} | collective-permute-start | bytes 1572872 | tf_op jit(solution)/shard_map/ppermute | solution.py:30
  31.2 7.3 %collective-permute-done.12.refs_0_ = bf16[128,2048]{1,0:T(8,128)(2,1)S(1)} collective-permute-done((bf16[128,2048]{1,0:T(8,128)(2,1)S(1)}, bf16[128,2048]{1,0:T(8,128)(2,1)S(1)}, u32[]{:S(2)}, u32[]{:S(2)}) %collective-permute-start.12) | collective-permute-done | bytes 524320 | tf_op jit(solution)/shard_map/ppermute | solution.py:30
  38.4 1.3 %collective-permute-start.8 = (bf16[128,2048]{1,0:T(8,128)(2,1)S(1)}, bf16[128,2048]{1,0:T(8,128)(2,1)S(1)}, u32[]{:S(2)}, u32[]{:S(2)}) collective-permute-start(bf16[128,2048]{1,0:T(8,128)(2,1)S(1)} %collective-permute-done.6.refs_8_), channel_id=1, source_target_pairs={{8,12},{12,8},{24,28},{28,24},{20,16},{9,13},{13,9},{25,29},{29,25... | collective-permute-start | bytes 1572872 | tf_op jit(solution)/shard_map/ppermute | solution.py:30
  39.7 0.4 collective-permute-done.7.refs_9_
  40.1 2.7 %collective-permute-start.9 = (bf16[128,2048]{1,0:T(8,128)(2,1)S(1)}, bf16[128,2048]{1,0:T(8,128)(2,1)S(1)}, u32[]{:S(2)}, u32[]{:S(2)}) collective-permute-start(bf16[128,2048]{1,0:T(8,128)(2,1)S(1)} %collective-permute-done.7.refs_9_), channel_id=1, source_target_pairs={{16,20},{17,21},{18,22},{19,23}} | collective-permute-start | bytes 1572872 | tf_op jit(solution)/shard_map/ppermute | solution.py:30
  42.8 0.0 collective-permute-done.11.refs_13_
  42.9 0.7 %collective-permute-start.14 = (bf16[128,2048]{1,0:T(8,128)(2,1)S(1)}, bf16[128,2048]{1,0:T(8,128)(2,1)S(1)}, u32[]{:S(2)}, u32[]{:S(2)}) collective-permute-start(bf16[128,2048]{1,0:T(8,128)(2,1)S(1)} %collective-permute-done.12.refs_0_), channel_id=1, source_target_pairs={{8,12},{12,8},{24,28},{28,24},{9,13},{13,9},{25,29},{29,25},{10,14... | collective-permute-start | bytes 1572872 | tf_op jit(solution)/shard_map/ppermute | solution.py:30
  43.6 5.3 %collective-permute-done.13.refs_1_ = bf16[128,2048]{1,0:T(8,128)(2,1)S(1)} collective-permute-done((bf16[128,2048]{1,0:T(8,128)(2,1)S(1)}, bf16[128,2048]{1,0:T(8,128)(2,1)S(1)}, u32[]{:S(2)}, u32[]{:S(2)}) %collective-permute-start.13) | collective-permute-done | bytes 524320 | tf_op jit(solution)/shard_map/ppermute | solution.py:30
  48.9 1.9 %collective-permute-start.15 = (bf16[128,2048]{1,0:T(8,128)(2,1)S(1)}, bf16[128,2048]{1,0:T(8,128)(2,1)S(1)}, u32[]{:S(2)}, u32[]{:S(2)}) collective-permute-start(bf16[128,2048]{1,0:T(8,128)(2,1)S(1)} %collective-permute-done.13.refs_1_), channel_id=1, source_target_pairs={{16,20},{20,16},{17,21},{21,17},{18,22},{22,18},{19,23},{23,19}} | collective-permute-start | bytes 1572872 | tf_op jit(solution)/shard_map/ppermute | solution.py:30
  50.8 0.0 collective-permute-done.10.refs_12_
  50.8 0.0 collective-permute-done.8.refs_10_
  50.8 0.0 collective-permute-done.9.refs_11_
  50.8 0.0 copy-done
  50.8 0.0 copy-done.1
  50.8 9.1 %shard_map.46 = (f32[8,2,512,256]{3,2,1,0:T(8,128)S(1)}, f32[8,2,512,128]{3,2,1,0:T(8,128)S(1)}) custom-call(s32[6]{0:T(128)S(1)} %copy-done.1, bf16[256,4096]{1,0:T(8,128)(2,1)S(1)} %copy-done, bf16[128,2048]{1,0:T(8,128)(2,1)S(1)} %pad_maximum_fusion.refs_0_, bf16[128,2048]{1,0:T(8,128)(2,1)S(1)} %pad_maximum_fusion.1.refs_1_, ...), custom_call_target="tpu_custom_call" | custom-call | flops 1879048192 | bytes 8388608 | tf_op jit(solution)/shard_map/pallas_call | solution.py:343
  60.0 0.0 collective-permute-done.14.refs_2_
  60.0 0.0 collective-permute-done.15.refs_3_
  60.0 6.5 %shard_map.47 = bf16[256,4096]{1,0:T(8,128)(2,1)} custom-call(s32[6]{0:T(128)S(1)} %copy-done.1, bf16[256,4096]{1,0:T(8,128)(2,1)S(1)} %copy-done, f32[8,2,512,256]{3,2,1,0:T(8,128)S(1)} %get-tuple-element.7.mixed_ref, f32[8,2,512,128]{3,2,1,0:T(8,128)S(1)} %get-tuple-element.8.top_ref, bf16[128,2048]{1,0:T(8,128)(2,1)S(1)} %collective-permute-done.12.refs_0_, ...), custom_call_target="tpu_custom_call" | custom-call | flops 536870912 | bytes 8388608 | tf_op jit(solution)/shard_map/pallas_call | solution.py:343
  (2 shorter events, 0.1 us)
Async XLA Ops:
  0.0 50.8 %copy-start = (bf16[256,4096]{1,0:T(8,128)(2,1)S(1)}, bf16[256,4096]{1,0:T(8,128)(2,1)}, u32[]{:S(2)}) copy-start(bf16[256,4096]{1,0:T(8,128)(2,1)} %q_all.3) | copy-start | bytes 6291460
  0.0 50.8 %copy-start.1 = (s32[6]{0:T(128)S(1)}, s32[6]{0:T(128)}, u32[]{:S(2)}) copy-start(s32[6]{0:T(128)} %docs_ref.3) | copy-start | bytes 76
  1.5 8.1 %collective-permute-start.2 = (bf16[128,2048]{1,0:T(8,128)(2,1)S(1)}, bf16[128,2048]{1,0:T(8,128)(2,1)S(1)}, u32[]{:S(2)}, u32[]{:S(2)}) collective-permute-start(bf16[128,2048]{1,0:T(8,128)(2,1)S(1)} %pad_maximum_fusion.refs_0_), channel_id=1, source_target_pairs={{12,24},{13,25},{14,26},{15,27}} | collective-permute-start | bytes 1572872 | tf_op jit(solution)/shard_map/ppermute | solution.py:30
  2.2 8.7 %collective-permute-start.3 = (bf16[128,2048]{1,0:T(8,128)(2,1)S(1)}, bf16[128,2048]{1,0:T(8,128)(2,1)S(1)}, u32[]{:S(2)}, u32[]{:S(2)}) collective-permute-start(bf16[128,2048]{1,0:T(8,128)(2,1)S(1)} %pad_maximum_fusion.1.refs_1_), channel_id=1, source_target_pairs={{8,24},{12,28},{9,25},{13,29},{10,26},{14,30},{11,27},{15,31}} | collective-permute-start | bytes 1572872 | tf_op jit(solution)/shard_map/ppermute | solution.py:30
  2.9 22.3 %collective-permute-start.5 = (bf16[128,2048]{1,0:T(8,128)(2,1)S(1)}, bf16[128,2048]{1,0:T(8,128)(2,1)S(1)}, u32[]{:S(2)}, u32[]{:S(2)}) collective-permute-start(bf16[128,2048]{1,0:T(8,128)(2,1)S(1)} %pad_maximum_fusion.1.refs_1_), channel_id=1, source_target_pairs={{0,16},{4,20},{1,17},{5,21},{2,18},{6,22},{3,19},{7,23}} | collective-permute-start | bytes 1572872 | tf_op jit(solution)/shard_map/ppermute | solution.py:30
  4.2 22.3 %collective-permute-start.6 = (bf16[128,2048]{1,0:T(8,128)(2,1)S(1)}, bf16[128,2048]{1,0:T(8,128)(2,1)S(1)}, u32[]{:S(2)}, u32[]{:S(2)}) collective-permute-start(bf16[128,2048]{1,0:T(8,128)(2,1)S(1)} %pad_maximum_fusion.refs_0_), channel_id=1, source_target_pairs={{0,8},{4,12},{16,24},{20,28},{8,20},{1,9},{5,13},{17,25},{21,29},{... | collective-permute-start | bytes 1572872 | tf_op jit(solution)/shard_map/ppermute | solution.py:30
  8.2 19.6 %collective-permute-start.1 = (bf16[128,2048]{1,0:T(8,128)(2,1)S(1)}, bf16[128,2048]{1,0:T(8,128)(2,1)S(1)}, u32[]{:S(2)}, u32[]{:S(2)}) collective-permute-start(bf16[128,2048]{1,0:T(8,128)(2,1)S(1)} %pad_maximum_fusion.1.refs_1_), channel_id=1, source_target_pairs={{0,4},{8,12},{16,20},{24,28},{1,5},{9,13},{17,21},{25,29},{2,6},{1... | collective-permute-start | bytes 1572872 | tf_op jit(solution)/shard_map/ppermute | solution.py:30
  9.6 19.0 %collective-permute-start = (bf16[128,2048]{1,0:T(8,128)(2,1)S(1)}, bf16[128,2048]{1,0:T(8,128)(2,1)S(1)}, u32[]{:S(2)}, u32[]{:S(2)}) collective-permute-start(bf16[128,2048]{1,0:T(8,128)(2,1)S(1)} %pad_maximum_fusion.refs_0_), channel_id=1, source_target_pairs={{0,4},{8,12},{16,20},{24,28},{1,5},{9,13},{17,21},{25,29},{2,6},{1... | collective-permute-start | bytes 1572872 | tf_op jit(solution)/shard_map/ppermute | solution.py:30
  10.9 18.9 %collective-permute-start.4 = (bf16[128,2048]{1,0:T(8,128)(2,1)S(1)}, bf16[128,2048]{1,0:T(8,128)(2,1)S(1)}, u32[]{:S(2)}, u32[]{:S(2)}) collective-permute-start(bf16[128,2048]{1,0:T(8,128)(2,1)S(1)} %pad_maximum_fusion.refs_0_), channel_id=1, source_target_pairs={{4,16},{5,17},{6,18},{7,19}} | collective-permute-start | bytes 1572872 | tf_op jit(solution)/shard_map/ppermute | solution.py:30
  25.2 13.2 %collective-permute-start.12 = (bf16[128,2048]{1,0:T(8,128)(2,1)S(1)}, bf16[128,2048]{1,0:T(8,128)(2,1)S(1)}, u32[]{:S(2)}, u32[]{:S(2)}) collective-permute-start(bf16[128,2048]{1,0:T(8,128)(2,1)S(1)} %pad_maximum_fusion.1.refs_1_), channel_id=1, source_target_pairs={{0,8},{4,12},{16,24},{20,28},{1,9},{5,13},{17,25},{21,29},{2,10},{... | collective-permute-start | bytes 1572872 | tf_op jit(solution)/shard_map/ppermute | solution.py:30
  26.5 13.6 %collective-permute-start.7 = (bf16[128,2048]{1,0:T(8,128)(2,1)S(1)}, bf16[128,2048]{1,0:T(8,128)(2,1)S(1)}, u32[]{:S(2)}, u32[]{:S(2)}) collective-permute-start(bf16[128,2048]{1,0:T(8,128)(2,1)S(1)} %collective-permute-done.2.refs_4_), channel_id=1, source_target_pairs={{24,16},{25,17},{26,18},{27,19}} | collective-permute-start | bytes 1572872 | tf_op jit(solution)/shard_map/ppermute | solution.py:30
  27.9 15.0 %collective-permute-start.11 = (bf16[128,2048]{1,0:T(8,128)(2,1)S(1)}, bf16[128,2048]{1,0:T(8,128)(2,1)S(1)}, u32[]{:S(2)}, u32[]{:S(2)}) collective-permute-start(bf16[128,2048]{1,0:T(8,128)(2,1)S(1)} %collective-permute-done.3.refs_5_), channel_id=1, source_target_pairs={{28,24},{29,25},{30,26},{31,27}} | collective-permute-start | bytes 1572872 | tf_op jit(solution)/shard_map/ppermute | solution.py:30
  28.6 20.3 %collective-permute-start.13 = (bf16[128,2048]{1,0:T(8,128)(2,1)S(1)}, bf16[128,2048]{1,0:T(8,128)(2,1)S(1)}, u32[]{:S(2)}, u32[]{:S(2)}) collective-permute-start(bf16[128,2048]{1,0:T(8,128)(2,1)S(1)} %collective-permute-done.3.refs_5_), channel_id=1, source_target_pairs={{24,16},{28,20},{25,17},{29,21},{26,18},{30,22},{27,19},{31,23}} | collective-permute-start | bytes 1572872 | tf_op jit(solution)/shard_map/ppermute | solution.py:30
  29.9 20.9 %collective-permute-start.10 = (bf16[128,2048]{1,0:T(8,128)(2,1)S(1)}, bf16[128,2048]{1,0:T(8,128)(2,1)S(1)}, u32[]{:S(2)}, u32[]{:S(2)}) collective-permute-start(bf16[128,2048]{1,0:T(8,128)(2,1)S(1)} %collective-permute-done.5.refs_7_), channel_id=1, source_target_pairs={{20,16},{21,17},{22,18},{23,19}} | collective-permute-start | bytes 1572872 | tf_op jit(solution)/shard_map/ppermute | solution.py:30
  38.4 12.3 %collective-permute-start.8 = (bf16[128,2048]{1,0:T(8,128)(2,1)S(1)}, bf16[128,2048]{1,0:T(8,128)(2,1)S(1)}, u32[]{:S(2)}, u32[]{:S(2)}) collective-permute-start(bf16[128,2048]{1,0:T(8,128)(2,1)S(1)} %collective-permute-done.6.refs_8_), channel_id=1, source_target_pairs={{8,12},{12,8},{24,28},{28,24},{20,16},{9,13},{13,9},{25,29},{29,25... | collective-permute-start | bytes 1572872 | tf_op jit(solution)/shard_map/ppermute | solution.py:30
  40.1 10.7 %collective-permute-start.9 = (bf16[128,2048]{1,0:T(8,128)(2,1)S(1)}, bf16[128,2048]{1,0:T(8,128)(2,1)S(1)}, u32[]{:S(2)}, u32[]{:S(2)}) collective-permute-start(bf16[128,2048]{1,0:T(8,128)(2,1)S(1)} %collective-permute-done.7.refs_9_), channel_id=1, source_target_pairs={{16,20},{17,21},{18,22},{19,23}} | collective-permute-start | bytes 1572872 | tf_op jit(solution)/shard_map/ppermute | solution.py:30
  42.9 17.1 %collective-permute-start.14 = (bf16[128,2048]{1,0:T(8,128)(2,1)S(1)}, bf16[128,2048]{1,0:T(8,128)(2,1)S(1)}, u32[]{:S(2)}, u32[]{:S(2)}) collective-permute-start(bf16[128,2048]{1,0:T(8,128)(2,1)S(1)} %collective-permute-done.12.refs_0_), channel_id=1, source_target_pairs={{8,12},{12,8},{24,28},{28,24},{9,13},{13,9},{25,29},{29,25},{10,14... | collective-permute-start | bytes 1572872 | tf_op jit(solution)/shard_map/ppermute | solution.py:30
  48.9 11.1 %collective-permute-start.15 = (bf16[128,2048]{1,0:T(8,128)(2,1)S(1)}, bf16[128,2048]{1,0:T(8,128)(2,1)S(1)}, u32[]{:S(2)}, u32[]{:S(2)}) collective-permute-start(bf16[128,2048]{1,0:T(8,128)(2,1)S(1)} %collective-permute-done.13.refs_1_), channel_id=1, source_target_pairs={{16,20},{20,16},{17,21},{21,17},{18,22},{22,18},{19,23},{23,19}} | collective-permute-start | bytes 1572872 | tf_op jit(solution)/shard_map/ppermute | solution.py:30

commit v2 on v1

--- a/solution.py
+++ b/solution.py
@@ -44,11 +44,8 @@
     a_high = high.to([(chip(1, b), chip(3, b)) for b in both])
     on_low = a_low.to([(chip(3, 0), chip(2, 0))])
     on_high = a_high.to([(chip(3, b), chip(2, b)) for b in both])
-    first = [
-        low,
-        high,
-        low.to(beside),
-        high.to(beside),
+    own = [low, high, low.to(beside), high.to(beside)]
+    middle = [
         a_low,
         a_high,
         b_low,
@@ -61,7 +58,7 @@
         a_high.to([(chip(3, 1), chip(3, 0))]),
     ]
     last = [near_high, on_high, near_high.to(swap(1, 3)), on_high.to(swap(2))]
-    return first, last
+    return own, middle, last
 
 
 def gather_exchange(own):
@@ -152,10 +149,6 @@
     return jnp.concatenate([scores[:, : (units - 1) * DOC_UNIT], last], axis=1)
 
 
-def twice(tile):
-    return jnp.concatenate([tile, tile], axis=1)
-
-
 def in_turn(jobs, start, finish):
     pending = start(jobs[0])
     for number, job in enumerate(jobs):
@@ -166,7 +159,7 @@
 
 
 CHUNK = 2
-FIRST_HEADS, LAST_HEADS = 4, 8
+FIRST_HEADS, MIDDLE_HEADS, LAST_HEADS = 4, 4, 8
 
 
 def unit_copies(pieces, slots, table, sems, buf, device, lowest, place):
@@ -194,30 +187,23 @@
 
 
 def first_kernel(plan, docs_ref, q_all, *refs):
-    slots, table, n_pieces, window, each, group, heads = plan
+    slots, table, n_pieces, _, each, group, heads = plan
     pieces = refs[:n_pieces]
     mixed_ref, top_ref, buf, sems = refs[n_pieces:]
     device = lax.axis_index("seq")
     first_unit = device * each
-    base = first_unit + each - window
-    late = late_units(device)
+    chip_unit = (device >> 1) * 2 * each
     columns = group * HEAD_DIM
-
-    def place(unit):
-        return unit - base - (unit > late[0]).astype(jnp.int32) - (unit > late[1]).astype(jnp.int32)
-
-    unit_copies(
-        pieces, slots, table, sems, buf, device, doc_start(docs_ref, first_unit), place
-    )()
+    place = lambda unit: unit - chip_unit
+    lowest = doc_start(docs_ref, first_unit)
+    unit_copies(pieces, slots, table, sems, buf, device, lowest, place)()
     steps = heads // FIRST_HEADS * each
 
     def one_step(step, carry):
         first_head, part = lax.div(step, each) * FIRST_HEADS, lax.rem(step, each)
         unit = first_unit + part
-        start = doc_start(docs_ref, unit)
-        skipped = sum(((u >= start) & (u <= unit)).astype(jnp.int32) for u in late)
-        here = unit - start + 1 - skipped
-        for units in range(1, window - each):
+        here = unit - jnp.maximum(doc_start(docs_ref, unit), chip_unit) + 1
+        for units in range(1, 2 * each + 1):
 
             @pl.when(here == units)
             def _():
@@ -239,6 +225,60 @@
                     mine = pl.ds(g * DOC_UNIT, CHUNK * DOC_UNIT)
                     mixed_ref[head, part, mine] = mixed(weights, buf[rows, columns_of(heads + head)])
                     top_ref[head, part, mine] = jnp.broadcast_to(top, (CHUNK * DOC_UNIT, HEAD_DIM))
+
+                in_turn(jobs, begin, end)
+
+        return carry
+
+    lax.fori_loop(0, steps, one_step, 0)
+
+
+def add_rows(old_mixed, old_top, scores, value_rows):
+    top = jnp.maximum(old_top, jnp.max(scores, axis=1, keepdims=True))
+    wide = jnp.concatenate([top] * (scores.shape[1] // HEAD_DIM), axis=1)
+    weights = jnp.exp2((scores - wide) * FACTOR)
+    shrink = jnp.exp2((old_top - top) * FACTOR)
+    both = jnp.concatenate([shrink, shrink], axis=1)
+    return old_mixed * both + mixed(weights, value_rows), top
+
+
+def middle_kernel(plan, docs_ref, q_all, old_mixed, old_top, *refs):
+    slots, table, n_pieces, window, each, group, heads = plan
+    pieces = refs[:n_pieces]
+    mixed_ref, top_ref, buf, sems = refs[n_pieces:]
+    device = lax.axis_index("seq")
+    first_unit = device * each
+    chip_unit = (device >> 1) * 2 * each
+    late = late_units(device)
+    columns = group * HEAD_DIM
+    most = window - each - 2
+    steps = heads // MIDDLE_HEADS * each
+    place = lambda unit: unit - (chip_unit - most - 2) - (unit > late[0]).astype(jnp.int32)
+    lowest = doc_start(docs_ref, first_unit)
+    unit_copies(pieces, slots, table, sems, buf, device, lowest, place)()
+
+    def one_step(step, carry):
+        first_head, part = lax.div(step, each) * MIDDLE_HEADS, lax.rem(step, each)
+        start = doc_start(docs_ref, first_unit + part)
+        here = chip_unit - start - sum((u >= start).astype(jnp.int32) for u in late)
+        for units in range(1, most + 1):
+
+            @pl.when(here == units)
+            def _():
+                rows = pl.ds((most - units) * DOC_UNIT, units * DOC_UNIT)
+                jobs = [(h, g) for h in range(MIDDLE_HEADS) for g in range(0, group, CHUNK)]
+
+                def begin(job):
+                    head, g = first_head + job[0], job[1]
+                    q = q_all[rows_of(part, 1), columns_of(head, columns)]
+                    return scores_of(stacked(q, range(g, g + CHUNK)), buf[rows, columns_of(head)])
+
+                def end(job, scores):
+                    head = first_head + job[0]
+                    at = (head, part, pl.ds(job[1] * DOC_UNIT, CHUNK * DOC_UNIT))
+                    mixed_ref[at], top_ref[at] = add_rows(
+                        old_mixed[at], old_top[at], scores, buf[rows, columns_of(heads + head)]
+                    )
 
                 in_turn(jobs, begin, end)
 
@@ -299,12 +339,10 @@
                 head = first_head + job[0]
                 column = lax.broadcasted_iota(jnp.int32, scores.shape, 1)
                 scores = jnp.where(column >= (2 - count) * DOC_UNIT, scores, -jnp.inf)
-                old = older(top_ref, job)
-                top = jnp.maximum(old, jnp.max(scores, axis=1, keepdims=True))
-                weights = jnp.exp2((scores - twice(top)) * FACTOR)
-                shrink = jnp.exp2((old - top) * FACTOR)
-                result = mixed(weights, buf[:, columns_of(heads + head)])
-                store(job, mean(older(mixed_ref, job) * twice(shrink) + result))
+                result, _ = add_rows(
+                    older(mixed_ref, job), older(top_ref, job), scores, buf[:, columns_of(heads + head)]
+                )
+                store(job, mean(result))
 
             in_turn(jobs, begin, end)
 
@@ -319,7 +357,7 @@
         copy_out(part).wait()
 
 
-def in_two(queries, doc_lengths, first, last, window, each, group, heads):
+def in_stages(queries, doc_lengths, first, middle, last, window, each, group, heads):
     rows = each * DOC_UNIT
     dtype = queries.dtype
     anywhere = pl.BlockSpec(memory_space=pl.ANY)
@@ -331,8 +369,9 @@
     )
     on_chip = pl.BlockSpec(memory_space=pltpu.VMEM)
     is_late = lambda device, unit: unit in late_units(device)
-
-    def call(kernel, pieces, wanted, held_rows, operands, in_specs, shapes, out_specs, scratch):
+    is_own = lambda device, unit: unit >= (device >> 1) * 2 * each
+
+    def call(kernel, pieces, wanted, held_rows, operands, in_specs, shapes, out_specs, scratch, aliases={}):
         slots, table = slots_of(pieces, window, each, wanted)
         plan = (slots, table, len(pieces), window, each, group, heads)
         scratch = [
@@ -350,6 +389,7 @@
                 out_specs=out_specs,
                 scratch_shapes=scratch,
             ),
+            input_output_aliases=aliases,
             compiler_params=pltpu.CompilerParams(vmem_limit_bytes=VMEM_LIMIT),
             cost_estimate=pl.CostEstimate(
                 flops=work, transcendentals=work // (4 * HEAD_DIM), bytes_accessed=4 * queries.size * 2
@@ -359,13 +399,25 @@
     so_far = call(
         first_kernel,
         first,
-        lambda device, unit: not is_late(device, unit),
-        (window - 2) * DOC_UNIT,
+        is_own,
+        2 * each * DOC_UNIT,
         (queries,),
         (on_chip,),
         state,
         (on_chip, on_chip),
         lambda n: [dma((n,))],
+    )
+    so_far = call(
+        middle_kernel,
+        middle,
+        lambda device, unit: not is_own(device, unit) and not is_late(device, unit),
+        (window - each - 2) * DOC_UNIT,
+        (queries, *so_far),
+        (on_chip, on_chip, on_chip),
+        state,
+        (on_chip, on_chip),
+        lambda n: [dma((n,))],
+        {2: 0, 3: 1},
     )
     return call(
         last_kernel,
@@ -577,8 +629,8 @@
             Piece(jnp.concatenate([keys[part], values[part]], axis=1), units[:, u : u + 1])
             for u, part in enumerate((slice(0, DOC_UNIT), slice(DOC_UNIT, rows)))
         )
-        first, last = cube_exchange(low, high)
-        return in_two(queries, doc_lengths, first, last, window, each, group, heads)
+        pieces = cube_exchange(low, high)
+        return in_stages(queries, doc_lengths, *pieces, window, each, group, heads)
     out = None
     parts = PARTS_OF_HEADS
     for part in range(parts):

time: 66.8 us -> 66.6 us (level)
  waiting for transfers between devices: 26 us -> 12.6 us
  starting transfers between devices: 23.1 us -> 32.2 us
  Pallas kernels: 15.6 us -> 19.5 us
    ppermute x16, waiting for transfers between devices: 26 us -> 12.6 us  [to(): return Piece(lax.ppermute(self.array, 'seq', pairs), units)]
    ppermute x16, starting transfers between devices: 23.1 us -> 32.2 us  [to(): return Piece(lax.ppermute(self.array, 'seq', pairs), units)]
    pallas_call x2 -> x3, Pallas kernels: 15.6 us -> 19.5 us  [call(): pl.pallas_call(functools.partial(kernel, plan), out_shape=shapes, grid_sp...]
  transfers between devices with their start and end apart: 16 -> 16, of which waited for: 4 -> 3; matrix products, arithmetic and copies ran while one was open for 0% -> 0% of each run, Pallas kernels for 14% -> 20%
where the time goes in v2:
time: 66.6 us; the launch traced here: 66.3 us
  starting transfers between devices  32.2 us (48%)
  Pallas kernels  19.5 us (29%)
  waiting for transfers between devices  12.6 us (19%)
  local copies, waits for them, and re-layouts  1.42 us (2%)
    ppermute x16, starting transfers between devices, to(): return Piece(lax.ppermute(self.array, 'seq', pairs), units)  32.2 us
    pallas_call x3, Pallas kernels, call(): pl.pallas_call(functools.partial(kernel, plan), out_shape=shapes, grid_sp...  19.5 us
    ppermute x16, waiting for transfers between devices, to(): return Piece(lax.ppermute(self.array, 'seq', pairs), units)  12.6 us
    slice x1, local copies, waits for them, and re-layouts, on_device(): keys[part]  1.41 us
  transfers between devices with their start and end apart: 16, of which 3 were waited for; matrix products, arithmetic and copies ran while one was open for 0% of the time, Pallas kernels for 20%

profile of v2, /device:TPU:12, one launch (start us, length us, event | category | flops | bytes accessed | tf_op | source)
XLA Modules:
  0.0 66.3 jit_solution(1892678857301136272)
XLA Ops:
  0.0 0.0 copy-start
  0.0 0.0 copy-start.1
  0.0 1.4 %fusion = (bf16[128,1024]{1,0:T(8,128)(2,1)S(1)}, bf16[128,1024]{1,0:T(8,128)(2,1)S(1)}, bf16[128,1024]{1,0:T(8,128)(2,1)S(1)}, bf16[128,1024]{1,0:T(8,128)(2,1)S(1)}) fusion(bf16[256,1024]{1,0:T(8,128)(2,1)} %param.5, bf16[256,1024]{1,0:T(8,128)(2,1)} %param.6), kind=kLoop, calls=%fused_computation.2 | loop fusion | bytes 2097152 | tf_op jit(solution)/shard_map/slice | solution.py:629
  1.5 1.8 %collective-permute-start.1 = (bf16[128,2048]{1,0:T(8,128)(2,1)S(1)}, bf16[128,2048]{1,0:T(8,128)(2,1)S(1)}, u32[]{:S(2)}, u32[]{:S(2)}) collective-permute-start(bf16[128,2048]{1,0:T(8,128)(2,1)S(1)} %pad_maximum_fusion.1.refs_1_), channel_id=1, source_target_pairs={{0,4},{8,12},{16,20},{24,28},{1,5},{9,13},{17,21},{25,29},{2,6},{1... | collective-permute-start | bytes 1572872 | tf_op jit(solution)/shard_map/ppermute | solution.py:30
  3.3 1.3 %collective-permute-start = (bf16[128,2048]{1,0:T(8,128)(2,1)S(1)}, bf16[128,2048]{1,0:T(8,128)(2,1)S(1)}, u32[]{:S(2)}, u32[]{:S(2)}) collective-permute-start(bf16[128,2048]{1,0:T(8,128)(2,1)S(1)} %pad_maximum_fusion.refs_0_), channel_id=1, source_target_pairs={{0,4},{8,12},{16,20},{24,28},{1,5},{9,13},{17,21},{25,29},{2,6},{1... | collective-permute-start | bytes 1572872 | tf_op jit(solution)/shard_map/ppermute | solution.py:30
  4.6 0.7 %collective-permute-start.2 = (bf16[128,2048]{1,0:T(8,128)(2,1)S(1)}, bf16[128,2048]{1,0:T(8,128)(2,1)S(1)}, u32[]{:S(2)}, u32[]{:S(2)}) collective-permute-start(bf16[128,2048]{1,0:T(8,128)(2,1)S(1)} %pad_maximum_fusion.refs_0_), channel_id=1, source_target_pairs={{12,24},{13,25},{14,26},{15,27}} | collective-permute-start | bytes 1572872 | tf_op jit(solution)/shard_map/ppermute | solution.py:30
  5.3 0.7 %collective-permute-start.3 = (bf16[128,2048]{1,0:T(8,128)(2,1)S(1)}, bf16[128,2048]{1,0:T(8,128)(2,1)S(1)}, u32[]{:S(2)}, u32[]{:S(2)}) collective-permute-start(bf16[128,2048]{1,0:T(8,128)(2,1)S(1)} %pad_maximum_fusion.1.refs_1_), channel_id=1, source_target_pairs={{8,24},{12,28},{9,25},{13,29},{10,26},{14,30},{11,27},{15,31}} | collective-permute-start | bytes 1572872 | tf_op jit(solution)/shard_map/ppermute | solution.py:30
  6.0 1.3 %collective-permute-start.5 = (bf16[128,2048]{1,0:T(8,128)(2,1)S(1)}, bf16[128,2048]{1,0:T(8,128)(2,1)S(1)}, u32[]{:S(2)}, u32[]{:S(2)}) collective-permute-start(bf16[128,2048]{1,0:T(8,128)(2,1)S(1)} %pad_maximum_fusion.1.refs_1_), channel_id=1, source_target_pairs={{0,16},{4,20},{1,17},{5,21},{2,18},{6,22},{3,19},{7,23}} | collective-permute-start | bytes 1572872 | tf_op jit(solution)/shard_map/ppermute | solution.py:30
  7.3 0.0 collective-permute-done.1.refs_3_
  7.3 4.0 %collective-permute-start.6 = (bf16[128,2048]{1,0:T(8,128)(2,1)S(1)}, bf16[128,2048]{1,0:T(8,128)(2,1)S(1)}, u32[]{:S(2)}, u32[]{:S(2)}) collective-permute-start(bf16[128,2048]{1,0:T(8,128)(2,1)S(1)} %pad_maximum_fusion.refs_0_), channel_id=1, source_target_pairs={{0,8},{4,12},{16,24},{20,28},{8,20},{1,9},{5,13},{17,25},{21,29},{... | collective-permute-start | bytes 1572872 | tf_op jit(solution)/shard_map/ppermute | solution.py:30
  11.4 0.0 collective-permute-done.refs_2_
  11.4 1.3 %collective-permute-start.4 = (bf16[128,2048]{1,0:T(8,128)(2,1)S(1)}, bf16[128,2048]{1,0:T(8,128)(2,1)S(1)}, u32[]{:S(2)}, u32[]{:S(2)}) collective-permute-start(bf16[128,2048]{1,0:T(8,128)(2,1)S(1)} %pad_maximum_fusion.refs_0_), channel_id=1, source_target_pairs={{4,16},{5,17},{6,18},{7,19}} | collective-permute-start | bytes 1572872 | tf_op jit(solution)/shard_map/ppermute | solution.py:30
  12.7 0.0 collective-permute-done.2.refs_0_
  12.7 9.6 %collective-permute-start.12 = (bf16[128,2048]{1,0:T(8,128)(2,1)S(1)}, bf16[128,2048]{1,0:T(8,128)(2,1)S(1)}, u32[]{:S(2)}, u32[]{:S(2)}) collective-permute-start(bf16[128,2048]{1,0:T(8,128)(2,1)S(1)} %pad_maximum_fusion.1.refs_1_), channel_id=1, source_target_pairs={{0,8},{4,12},{16,24},{20,28},{1,9},{5,13},{17,25},{21,29},{2,10},{... | collective-permute-start | bytes 1572872 | tf_op jit(solution)/shard_map/ppermute | solution.py:30
  22.3 0.0 collective-permute-done.3.refs_1_
  22.3 1.3 %collective-permute-start.7 = (bf16[128,2048]{1,0:T(8,128)(2,1)S(1)}, bf16[128,2048]{1,0:T(8,128)(2,1)S(1)}, u32[]{:S(2)}, u32[]{:S(2)}) collective-permute-start(bf16[128,2048]{1,0:T(8,128)(2,1)S(1)} %collective-permute-done.2.refs_0_), channel_id=1, source_target_pairs={{24,16},{25,17},{26,18},{27,19}} | collective-permute-start | bytes 1572872 | tf_op jit(solution)/shard_map/ppermute | solution.py:30
  23.6 4.7 %collective-permute-done.5.refs_3_ = bf16[128,2048]{1,0:T(8,128)(2,1)S(1)} collective-permute-done((bf16[128,2048]{1,0:T(8,128)(2,1)S(1)}, bf16[128,2048]{1,0:T(8,128)(2,1)S(1)}, u32[]{:S(2)}, u32[]{:S(2)}) %collective-permute-start.5) | collective-permute-done | bytes 524320 | tf_op jit(solution)/shard_map/ppermute | solution.py:30
  28.3 0.7 %collective-permute-start.11 = (bf16[128,2048]{1,0:T(8,128)(2,1)S(1)}, bf16[128,2048]{1,0:T(8,128)(2,1)S(1)}, u32[]{:S(2)}, u32[]{:S(2)}) collective-permute-start(bf16[128,2048]{1,0:T(8,128)(2,1)S(1)} %collective-permute-done.3.refs_1_), channel_id=1, source_target_pairs={{28,24},{29,25},{30,26},{31,27}} | collective-permute-start | bytes 1572872 | tf_op jit(solution)/shard_map/ppermute | solution.py:30
  29.0 0.0 collective-permute-done.6.refs_4_
  29.0 1.3 %collective-permute-start.13 = (bf16[128,2048]{1,0:T(8,128)(2,1)S(1)}, bf16[128,2048]{1,0:T(8,128)(2,1)S(1)}, u32[]{:S(2)}, u32[]{:S(2)}) collective-permute-start(bf16[128,2048]{1,0:T(8,128)(2,1)S(1)} %collective-permute-done.3.refs_1_), channel_id=1, source_target_pairs={{24,16},{28,20},{25,17},{29,21},{26,18},{30,22},{27,19},{31,23}} | collective-permute-start | bytes 1572872 | tf_op jit(solution)/shard_map/ppermute | solution.py:30
  30.3 2.0 %collective-permute-done.4.refs_2_ = bf16[128,2048]{1,0:T(8,128)(2,1)S(1)} collective-permute-done((bf16[128,2048]{1,0:T(8,128)(2,1)S(1)}, bf16[128,2048]{1,0:T(8,128)(2,1)S(1)}, u32[]{:S(2)}, u32[]{:S(2)}) %collective-permute-start.4) | collective-permute-done | bytes 524320 | tf_op jit(solution)/shard_map/ppermute | solution.py:30
  32.3 1.3 %collective-permute-start.10 = (bf16[128,2048]{1,0:T(8,128)(2,1)S(1)}, bf16[128,2048]{1,0:T(8,128)(2,1)S(1)}, u32[]{:S(2)}, u32[]{:S(2)}) collective-permute-start(bf16[128,2048]{1,0:T(8,128)(2,1)S(1)} %collective-permute-done.5.refs_3_), channel_id=1, source_target_pairs={{20,16},{21,17},{22,18},{23,19}} | collective-permute-start | bytes 1572872 | tf_op jit(solution)/shard_map/ppermute | solution.py:30
  33.6 0.0 collective-permute-done.12.refs_0_
  33.6 1.3 %collective-permute-start.8 = (bf16[128,2048]{1,0:T(8,128)(2,1)S(1)}, bf16[128,2048]{1,0:T(8,128)(2,1)S(1)}, u32[]{:S(2)}, u32[]{:S(2)}) collective-permute-start(bf16[128,2048]{1,0:T(8,128)(2,1)S(1)} %collective-permute-done.6.refs_4_), channel_id=1, source_target_pairs={{8,12},{12,8},{24,28},{28,24},{20,16},{9,13},{13,9},{25,29},{29,25... | collective-permute-start | bytes 1572872 | tf_op jit(solution)/shard_map/ppermute | solution.py:30
  34.9 0.0 collective-permute-done.7.refs_5_
  34.9 3.1 %collective-permute-start.9 = (bf16[128,2048]{1,0:T(8,128)(2,1)S(1)}, bf16[128,2048]{1,0:T(8,128)(2,1)S(1)}, u32[]{:S(2)}, u32[]{:S(2)}) collective-permute-start(bf16[128,2048]{1,0:T(8,128)(2,1)S(1)} %collective-permute-done.7.refs_5_), channel_id=1, source_target_pairs={{16,20},{17,21},{18,22},{19,23}} | collective-permute-start | bytes 1572872 | tf_op jit(solution)/shard_map/ppermute | solution.py:30
  38.0 0.0 collective-permute-done.11.refs_9_
  38.1 0.7 %collective-permute-start.14 = (bf16[128,2048]{1,0:T(8,128)(2,1)S(1)}, bf16[128,2048]{1,0:T(8,128)(2,1)S(1)}, u32[]{:S(2)}, u32[]{:S(2)}) collective-permute-start(bf16[128,2048]{1,0:T(8,128)(2,1)S(1)} %collective-permute-done.12.refs_0_), channel_id=1, source_target_pairs={{8,12},{12,8},{24,28},{28,24},{9,13},{13,9},{25,29},{29,25},{10,14... | collective-permute-start | bytes 1572872 | tf_op jit(solution)/shard_map/ppermute | solution.py:30
  38.8 5.8 %collective-permute-done.13.refs_1_ = bf16[128,2048]{1,0:T(8,128)(2,1)S(1)} collective-permute-done((bf16[128,2048]{1,0:T(8,128)(2,1)S(1)}, bf16[128,2048]{1,0:T(8,128)(2,1)S(1)}, u32[]{:S(2)}, u32[]{:S(2)}) %collective-permute-start.13) | collective-permute-done | bytes 524320 | tf_op jit(solution)/shard_map/ppermute | solution.py:30
  44.6 1.9 %collective-permute-start.15 = (bf16[128,2048]{1,0:T(8,128)(2,1)S(1)}, bf16[128,2048]{1,0:T(8,128)(2,1)S(1)}, u32[]{:S(2)}, u32[]{:S(2)}) collective-permute-start(bf16[128,2048]{1,0:T(8,128)(2,1)S(1)} %collective-permute-done.13.refs_1_), channel_id=1, source_target_pairs={{16,20},{20,16},{17,21},{21,17},{18,22},{22,18},{19,23},{23,19}} | collective-permute-start | bytes 1572872 | tf_op jit(solution)/shard_map/ppermute | solution.py:30
  46.5 0.0 copy-done
  46.5 0.0 copy-done.1
  46.5 4.8 %shard_map.46 = (f32[8,2,512,256]{3,2,1,0:T(8,128)S(1)}, f32[8,2,512,128]{3,2,1,0:T(8,128)S(1)}) custom-call(s32[6]{0:T(128)S(1)} %copy-done.1, bf16[256,4096]{1,0:T(8,128)(2,1)S(1)} %copy-done, bf16[128,2048]{1,0:T(8,128)(2,1)S(1)} %pad_maximum_fusion.refs_0_, bf16[128,2048]{1,0:T(8,128)(2,1)S(1)} %pad_maximum_fusion.1.refs_1_, ...), custom_call_target="tpu_custom_call" | custom-call | flops 1073741824 | bytes 8388608 | tf_op jit(solution)/shard_map/pallas_call | solution.py:382
  51.3 0.0 collective-permute-done.10.refs_8_
  51.3 0.0 collective-permute-done.8.refs_6_
  51.4 0.0 collective-permute-done.9.refs_7_
  51.4 8.2 %shard_map.47 = (f32[8,2,512,256]{3,2,1,0:T(8,128)S(1)}, f32[8,2,512,128]{3,2,1,0:T(8,128)S(1)}) custom-call(s32[6]{0:T(128)S(1)} %copy-done.1, bf16[256,4096]{1,0:T(8,128)(2,1)S(1)} %copy-done, f32[8,2,512,256]{3,2,1,0:T(8,128)S(1)} %get-tuple-element.9.old_mixed, ...), custom_call_target="tpu_custom_call", output_to_operand_aliasing={{0}: (2, {}), {1}: (3, {})} | custom-call | flops 1342177280 | bytes 8388608 | tf_op jit(solution)/shard_map/pallas_call | solution.py:382
  59.6 0.0 collective-permute-done.14.refs_2_
  59.6 0.0 collective-permute-done.15.refs_3_
  59.6 6.5 %shard_map.48 = bf16[256,4096]{1,0:T(8,128)(2,1)} custom-call(s32[6]{0:T(128)S(1)} %copy-done.1, bf16[256,4096]{1,0:T(8,128)(2,1)S(1)} %copy-done, f32[8,2,512,256]{3,2,1,0:T(8,128)S(1)} %get-tuple-element.11.mixed_ref, f32[8,2,512,128]{3,2,1,0:T(8,128)S(1)} %get-tuple-element.12.top_ref, bf16[128,2048]{1,0:T(8,128)(2,1)S(1)} %collective-permute-done.12.refs_0_, ...), custom_call_target="tpu_custom_call" | custom-call | flops 536870912 | bytes 8388608 | tf_op jit(solution)/shard_map/pallas_call | solution.py:382
  (2 shorter events, 0.1 us)
Async XLA Ops:
  0.0 46.5 %copy-start = (bf16[256,4096]{1,0:T(8,128)(2,1)S(1)}, bf16[256,4096]{1,0:T(8,128)(2,1)}, u32[]{:S(2)}) copy-start(bf16[256,4096]{1,0:T(8,128)(2,1)} %q_all.5) | copy-start | bytes 6291460
  0.0 46.5 %copy-start.1 = (s32[6]{0:T(128)S(1)}, s32[6]{0:T(128)}, u32[]{:S(2)}) copy-start(s32[6]{0:T(128)} %docs_ref.5) | copy-start | bytes 76
  1.5 5.9 %collective-permute-start.1 = (bf16[128,2048]{1,0:T(8,128)(2,1)S(1)}, bf16[128,2048]{1,0:T(8,128)(2,1)S(1)}, u32[]{:S(2)}, u32[]{:S(2)}) collective-permute-start(bf16[128,2048]{1,0:T(8,128)(2,1)S(1)} %pad_maximum_fusion.1.refs_1_), channel_id=1, source_target_pairs={{0,4},{8,12},{16,20},{24,28},{1,5},{9,13},{17,21},{25,29},{2,6},{1... | collective-permute-start | bytes 1572872 | tf_op jit(solution)/shard_map/ppermute | solution.py:30
  3.3 8.1 %collective-permute-start = (bf16[128,2048]{1,0:T(8,128)(2,1)S(1)}, bf16[128,2048]{1,0:T(8,128)(2,1)S(1)}, u32[]{:S(2)}, u32[]{:S(2)}) collective-permute-start(bf16[128,2048]{1,0:T(8,128)(2,1)S(1)} %pad_maximum_fusion.refs_0_), channel_id=1, source_target_pairs={{0,4},{8,12},{16,20},{24,28},{1,5},{9,13},{17,21},{25,29},{2,6},{1... | collective-permute-start | bytes 1572872 | tf_op jit(solution)/shard_map/ppermute | solution.py:30
  4.6 8.1 %collective-permute-start.2 = (bf16[128,2048]{1,0:T(8,128)(2,1)S(1)}, bf16[128,2048]{1,0:T(8,128)(2,1)S(1)}, u32[]{:S(2)}, u32[]{:S(2)}) collective-permute-start(bf16[128,2048]{1,0:T(8,128)(2,1)S(1)} %pad_maximum_fusion.refs_0_), channel_id=1, source_target_pairs={{12,24},{13,25},{14,26},{15,27}} | collective-permute-start | bytes 1572872 | tf_op jit(solution)/shard_map/ppermute | solution.py:30
  5.3 17.0 %collective-permute-start.3 = (bf16[128,2048]{1,0:T(8,128)(2,1)S(1)}, bf16[128,2048]{1,0:T(8,128)(2,1)S(1)}, u32[]{:S(2)}, u32[]{:S(2)}) collective-permute-start(bf16[128,2048]{1,0:T(8,128)(2,1)S(1)} %pad_maximum_fusion.1.refs_1_), channel_id=1, source_target_pairs={{8,24},{12,28},{9,25},{13,29},{10,26},{14,30},{11,27},{15,31}} | collective-permute-start | bytes 1572872 | tf_op jit(solution)/shard_map/ppermute | solution.py:30
  6.0 22.3 %collective-permute-start.5 = (bf16[128,2048]{1,0:T(8,128)(2,1)S(1)}, bf16[128,2048]{1,0:T(8,128)(2,1)S(1)}, u32[]{:S(2)}, u32[]{:S(2)}) collective-permute-start(bf16[128,2048]{1,0:T(8,128)(2,1)S(1)} %pad_maximum_fusion.1.refs_1_), channel_id=1, source_target_pairs={{0,16},{4,20},{1,17},{5,21},{2,18},{6,22},{3,19},{7,23}} | collective-permute-start | bytes 1572872 | tf_op jit(solution)/shard_map/ppermute | solution.py:30
  7.3 21.7 %collective-permute-start.6 = (bf16[128,2048]{1,0:T(8,128)(2,1)S(1)}, bf16[128,2048]{1,0:T(8,128)(2,1)S(1)}, u32[]{:S(2)}, u32[]{:S(2)}) collective-permute-start(bf16[128,2048]{1,0:T(8,128)(2,1)S(1)} %pad_maximum_fusion.refs_0_), channel_id=1, source_target_pairs={{0,8},{4,12},{16,24},{20,28},{8,20},{1,9},{5,13},{17,25},{21,29},{... | collective-permute-start | bytes 1572872 | tf_op jit(solution)/shard_map/ppermute | solution.py:30
  11.4 20.9 %collective-permute-start.4 = (bf16[128,2048]{1,0:T(8,128)(2,1)S(1)}, bf16[128,2048]{1,0:T(8,128)(2,1)S(1)}, u32[]{:S(2)}, u32[]{:S(2)}) collective-permute-start(bf16[128,2048]{1,0:T(8,128)(2,1)S(1)} %pad_maximum_fusion.refs_0_), channel_id=1, source_target_pairs={{4,16},{5,17},{6,18},{7,19}} | collective-permute-start | bytes 1572872 | tf_op jit(solution)/shard_map/ppermute | solution.py:30
  12.7 20.9 %collective-permute-start.12 = (bf16[128,2048]{1,0:T(8,128)(2,1)S(1)}, bf16[128,2048]{1,0:T(8,128)(2,1)S(1)}, u32[]{:S(2)}, u32[]{:S(2)}) collective-permute-start(bf16[128,2048]{1,0:T(8,128)(2,1)S(1)} %pad_maximum_fusion.1.refs_1_), channel_id=1, source_target_pairs={{0,8},{4,12},{16,24},{20,28},{1,9},{5,13},{17,25},{21,29},{2,10},{... | collective-permute-start | bytes 1572872 | tf_op jit(solution)/shard_map/ppermute | solution.py:30
  22.3 12.6 %collective-permute-start.7 = (bf16[128,2048]{1,0:T(8,128)(2,1)S(1)}, bf16[128,2048]{1,0:T(8,128)(2,1)S(1)}, u32[]{:S(2)}, u32[]{:S(2)}) collective-permute-start(bf16[128,2048]{1,0:T(8,128)(2,1)S(1)} %collective-permute-done.2.refs_0_), channel_id=1, source_target_pairs={{24,16},{25,17},{26,18},{27,19}} | collective-permute-start | bytes 1572872 | tf_op jit(solution)/shard_map/ppermute | solution.py:30
  28.3 9.7 %collective-permute-start.11 = (bf16[128,2048]{1,0:T(8,128)(2,1)S(1)}, bf16[128,2048]{1,0:T(8,128)(2,1)S(1)}, u32[]{:S(2)}, u32[]{:S(2)}) collective-permute-start(bf16[128,2048]{1,0:T(8,128)(2,1)S(1)} %collective-permute-done.3.refs_1_), channel_id=1, source_target_pairs={{28,24},{29,25},{30,26},{31,27}} | collective-permute-start | bytes 1572872 | tf_op jit(solution)/shard_map/ppermute | solution.py:30
  29.0 15.6 %collective-permute-start.13 = (bf16[128,2048]{1,0:T(8,128)(2,1)S(1)}, bf16[128,2048]{1,0:T(8,128)(2,1)S(1)}, u32[]{:S(2)}, u32[]{:S(2)}) collective-permute-start(bf16[128,2048]{1,0:T(8,128)(2,1)S(1)} %collective-permute-done.3.refs_1_), channel_id=1, source_target_pairs={{24,16},{28,20},{25,17},{29,21},{26,18},{30,22},{27,19},{31,23}} | collective-permute-start | bytes 1572872 | tf_op jit(solution)/shard_map/ppermute | solution.py:30
  32.3 19.0 %collective-permute-start.10 = (bf16[128,2048]{1,0:T(8,128)(2,1)S(1)}, bf16[128,2048]{1,0:T(8,128)(2,1)S(1)}, u32[]{:S(2)}, u32[]{:S(2)}) collective-permute-start(bf16[128,2048]{1,0:T(8,128)(2,1)S(1)} %collective-permute-done.5.refs_3_), channel_id=1, source_target_pairs={{20,16},{21,17},{22,18},{23,19}} | collective-permute-start | bytes 1572872 | tf_op jit(solution)/shard_map/ppermute | solution.py:30
  33.6 17.7 %collective-permute-start.8 = (bf16[128,2048]{1,0:T(8,128)(2,1)S(1)}, bf16[128,2048]{1,0:T(8,128)(2,1)S(1)}, u32[]{:S(2)}, u32[]{:S(2)}) collective-permute-start(bf16[128,2048]{1,0:T(8,128)(2,1)S(1)} %collective-permute-done.6.refs_4_), channel_id=1, source_target_pairs={{8,12},{12,8},{24,28},{28,24},{20,16},{9,13},{13,9},{25,29},{29,25... | collective-permute-start | bytes 1572872 | tf_op jit(solution)/shard_map/ppermute | solution.py:30
  34.9 16.4 %collective-permute-start.9 = (bf16[128,2048]{1,0:T(8,128)(2,1)S(1)}, bf16[128,2048]{1,0:T(8,128)(2,1)S(1)}, u32[]{:S(2)}, u32[]{:S(2)}) collective-permute-start(bf16[128,2048]{1,0:T(8,128)(2,1)S(1)} %collective-permute-done.7.refs_5_), channel_id=1, source_target_pairs={{16,20},{17,21},{18,22},{19,23}} | collective-permute-start | bytes 1572872 | tf_op jit(solution)/shard_map/ppermute | solution.py:30
  38.1 21.6 %collective-permute-start.14 = (bf16[128,2048]{1,0:T(8,128)(2,1)S(1)}, bf16[128,2048]{1,0:T(8,128)(2,1)S(1)}, u32[]{:S(2)}, u32[]{:S(2)}) collective-permute-start(bf16[128,2048]{1,0:T(8,128)(2,1)S(1)} %collective-permute-done.12.refs_0_), channel_id=1, source_target_pairs={{8,12},{12,8},{24,28},{28,24},{9,13},{13,9},{25,29},{29,25},{10,14... | collective-permute-start | bytes 1572872 | tf_op jit(solution)/shard_map/ppermute | solution.py:30
  44.6 15.0 %collective-permute-start.15 = (bf16[128,2048]{1,0:T(8,128)(2,1)S(1)}, bf16[128,2048]{1,0:T(8,128)(2,1)S(1)}, u32[]{:S(2)}, u32[]{:S(2)}) collective-permute-start(bf16[128,2048]{1,0:T(8,128)(2,1)S(1)} %collective-permute-done.13.refs_1_), channel_id=1, source_target_pairs={{16,20},{20,16},{17,21},{21,17},{18,22},{22,18},{19,23},{23,19}} | collective-permute-start | bytes 1572872 | tf_op jit(solution)/shard_map/ppermute | solution.py:30

commit v3 on v2

--- a/solution.py
+++ b/solution.py
@@ -158,7 +158,7 @@
         finish(job, started)
 
 
-CHUNK = 2
+CHUNK = 4
 FIRST_HEADS, MIDDLE_HEADS, LAST_HEADS = 4, 4, 8
 
 
@@ -299,9 +299,10 @@
     place = lambda unit: (unit > late[0]).astype(jnp.int32)
     unit_copies(pieces, slots, table, sems, buf, device, 0, place)()
 
-    def copy_out(part):
-        there = rows_of(part, 1)
-        return pltpu.make_async_copy(out_all.at[there], out_hbm.at[there], out_sems.at[part])
+    def copy_out(step):
+        part, which = lax.rem(step, each), lax.div(step, each)
+        there = (rows_of(part, 1), columns_of(which, LAST_HEADS * columns))
+        return pltpu.make_async_copy(out_all.at[there], out_hbm.at[there], out_sems.at[step])
 
     def one_step(step, carry):
         part, first_head = lax.rem(step, each), lax.div(step, each) * LAST_HEADS
@@ -328,33 +329,31 @@
             for job in jobs:
                 store(job, mean(older(mixed_ref, job)))
 
-        @pl.when(count > 0)
-        def _():
-            def begin(job):
-                head = first_head + job[0]
-                q = q_all[rows_of(part, 1), columns_of(head, columns)]
-                return scores_of(stacked(q, range(job[1], job[1] + CHUNK)), buf[:, columns_of(head)])
-
-            def end(job, scores):
-                head = first_head + job[0]
-                column = lax.broadcasted_iota(jnp.int32, scores.shape, 1)
-                scores = jnp.where(column >= (2 - count) * DOC_UNIT, scores, -jnp.inf)
-                result, _ = add_rows(
-                    older(mixed_ref, job), older(top_ref, job), scores, buf[:, columns_of(heads + head)]
-                )
-                store(job, mean(result))
-
-            in_turn(jobs, begin, end)
-
-        @pl.when(first_head == heads - LAST_HEADS)
-        def _():
-            copy_out(part).start()
-
+        for units in (1, 2):
+
+            @pl.when(count == units)
+            def _():
+                rows = pl.ds((2 - units) * DOC_UNIT, units * DOC_UNIT)
+
+                def begin(job):
+                    head = first_head + job[0]
+                    q = q_all[rows_of(part, 1), columns_of(head, columns)]
+                    heads_here = range(job[1], job[1] + CHUNK)
+                    return scores_of(stacked(q, heads_here), buf[rows, columns_of(head)])
+
+                def end(job, scores):
+                    value_rows = buf[rows, columns_of(heads + first_head + job[0])]
+                    state = older(mixed_ref, job), older(top_ref, job)
+                    store(job, mean(add_rows(*state, scores, value_rows)[0]))
+
+                in_turn(jobs, begin, end)
+
+        copy_out(step).start()
         return carry
 
     lax.fori_loop(0, steps, one_step, 0)
-    for part in range(each):
-        copy_out(part).wait()
+    for step in range(steps):
+        copy_out(step).wait()
 
 
 def in_stages(queries, doc_lengths, first, middle, last, window, each, group, heads):
@@ -428,7 +427,7 @@
         (on_chip, on_chip, on_chip),
         jax.ShapeDtypeStruct(queries.shape, dtype),
         anywhere,
-        lambda n: [pltpu.VMEM(queries.shape, dtype), dma((n,)), dma((each,))],
+        lambda n: [pltpu.VMEM(queries.shape, dtype), dma((n,)), dma((heads // LAST_HEADS * each,))],
     )
 
 

time: 66.6 us -> 65.3 us (0.980)
  Pallas kernels: 19.5 us -> 18.2 us
    pallas_call x3, Pallas kernels: 19.5 us -> 18.2 us  [call(): pl.pallas_call(functools.partial(kernel, plan), out_shape=shapes, grid_sp...]
  transfers between devices with their start and end apart: 16 -> 16, of which waited for: 3 -> 3; matrix products, arithmetic and copies ran while one was open for 0% -> 0% of each run, Pallas kernels for 20% -> 19%
where the time goes in v3:
time: 65.3 us; the launch traced here: 65 us
  starting transfers between devices  32.2 us (49%)
  Pallas kernels  18.2 us (28%)
  waiting for transfers between devices  12.6 us (19%)
  local copies, waits for them, and re-layouts  1.42 us (2%)
    ppermute x16, starting transfers between devices, to(): return Piece(lax.ppermute(self.array, 'seq', pairs), units)  32.2 us
    pallas_call x3, Pallas kernels, call(): pl.pallas_call(functools.partial(kernel, plan), out_shape=shapes, grid_sp...  18.2 us
    ppermute x16, waiting for transfers between devices, to(): return Piece(lax.ppermute(self.array, 'seq', pairs), units)  12.6 us
    slice x1, local copies, waits for them, and re-layouts, on_device(): keys[part]  1.41 us
  transfers between devices with their start and end apart: 16, of which 3 were waited for; matrix products, arithmetic and copies ran while one was open for 0% of the time, Pallas kernels for 19%

profile of v3, /device:TPU:12, one launch (start us, length us, event | category | flops | bytes accessed | tf_op | source)
XLA Modules:
  0.0 65.0 jit_solution(8876856702465044076)
XLA Ops:
  0.0 0.0 copy-start
  0.0 0.0 copy-start.1
  0.0 1.4 %fusion = (bf16[128,1024]{1,0:T(8,128)(2,1)S(1)}, bf16[128,1024]{1,0:T(8,128)(2,1)S(1)}, bf16[128,1024]{1,0:T(8,128)(2,1)S(1)}, bf16[128,1024]{1,0:T(8,128)(2,1)S(1)}) fusion(bf16[256,1024]{1,0:T(8,128)(2,1)} %param.5, bf16[256,1024]{1,0:T(8,128)(2,1)} %param.6), kind=kLoop, calls=%fused_computation.2 | loop fusion | bytes 2097152 | tf_op jit(solution)/shard_map/slice | solution.py:628
  1.5 1.8 %collective-permute-start.1 = (bf16[128,2048]{1,0:T(8,128)(2,1)S(1)}, bf16[128,2048]{1,0:T(8,128)(2,1)S(1)}, u32[]{:S(2)}, u32[]{:S(2)}) collective-permute-start(bf16[128,2048]{1,0:T(8,128)(2,1)S(1)} %pad_maximum_fusion.1.refs_1_), channel_id=1, source_target_pairs={{0,4},{8,12},{16,20},{24,28},{1,5},{9,13},{17,21},{25,29},{2,6},{1... | collective-permute-start | bytes 1572872 | tf_op jit(solution)/shard_map/ppermute | solution.py:30
  3.3 1.3 %collective-permute-start = (bf16[128,2048]{1,0:T(8,128)(2,1)S(1)}, bf16[128,2048]{1,0:T(8,128)(2,1)S(1)}, u32[]{:S(2)}, u32[]{:S(2)}) collective-permute-start(bf16[128,2048]{1,0:T(8,128)(2,1)S(1)} %pad_maximum_fusion.refs_0_), channel_id=1, source_target_pairs={{0,4},{8,12},{16,20},{24,28},{1,5},{9,13},{17,21},{25,29},{2,6},{1... | collective-permute-start | bytes 1572872 | tf_op jit(solution)/shard_map/ppermute | solution.py:30
  4.6 0.7 %collective-permute-start.2 = (bf16[128,2048]{1,0:T(8,128)(2,1)S(1)}, bf16[128,2048]{1,0:T(8,128)(2,1)S(1)}, u32[]{:S(2)}, u32[]{:S(2)}) collective-permute-start(bf16[128,2048]{1,0:T(8,128)(2,1)S(1)} %pad_maximum_fusion.refs_0_), channel_id=1, source_target_pairs={{12,24},{13,25},{14,26},{15,27}} | collective-permute-start | bytes 1572872 | tf_op jit(solution)/shard_map/ppermute | solution.py:30
  5.3 0.7 %collective-permute-start.3 = (bf16[128,2048]{1,0:T(8,128)(2,1)S(1)}, bf16[128,2048]{1,0:T(8,128)(2,1)S(1)}, u32[]{:S(2)}, u32[]{:S(2)}) collective-permute-start(bf16[128,2048]{1,0:T(8,128)(2,1)S(1)} %pad_maximum_fusion.1.refs_1_), channel_id=1, source_target_pairs={{8,24},{12,28},{9,25},{13,29},{10,26},{14,30},{11,27},{15,31}} | collective-permute-start | bytes 1572872 | tf_op jit(solution)/shard_map/ppermute | solution.py:30
  6.0 1.3 %collective-permute-start.5 = (bf16[128,2048]{1,0:T(8,128)(2,1)S(1)}, bf16[128,2048]{1,0:T(8,128)(2,1)S(1)}, u32[]{:S(2)}, u32[]{:S(2)}) collective-permute-start(bf16[128,2048]{1,0:T(8,128)(2,1)S(1)} %pad_maximum_fusion.1.refs_1_), channel_id=1, source_target_pairs={{0,16},{4,20},{1,17},{5,21},{2,18},{6,22},{3,19},{7,23}} | collective-permute-start | bytes 1572872 | tf_op jit(solution)/shard_map/ppermute | solution.py:30
  7.3 0.0 collective-permute-done.1.refs_3_
  7.3 4.0 %collective-permute-start.6 = (bf16[128,2048]{1,0:T(8,128)(2,1)S(1)}, bf16[128,2048]{1,0:T(8,128)(2,1)S(1)}, u32[]{:S(2)}, u32[]{:S(2)}) collective-permute-start(bf16[128,2048]{1,0:T(8,128)(2,1)S(1)} %pad_maximum_fusion.refs_0_), channel_id=1, source_target_pairs={{0,8},{4,12},{16,24},{20,28},{8,20},{1,9},{5,13},{17,25},{21,29},{... | collective-permute-start | bytes 1572872 | tf_op jit(solution)/shard_map/ppermute | solution.py:30
  11.4 0.0 collective-permute-done.refs_2_
  11.4 1.3 %collective-permute-start.4 = (bf16[128,2048]{1,0:T(8,128)(2,1)S(1)}, bf16[128,2048]{1,0:T(8,128)(2,1)S(1)}, u32[]{:S(2)}, u32[]{:S(2)}) collective-permute-start(bf16[128,2048]{1,0:T(8,128)(2,1)S(1)} %pad_maximum_fusion.refs_0_), channel_id=1, source_target_pairs={{4,16},{5,17},{6,18},{7,19}} | collective-permute-start | bytes 1572872 | tf_op jit(solution)/shard_map/ppermute | solution.py:30
  12.7 0.0 collective-permute-done.2.refs_0_
  12.7 9.6 %collective-permute-start.12 = (bf16[128,2048]{1,0:T(8,128)(2,1)S(1)}, bf16[128,2048]{1,0:T(8,128)(2,1)S(1)}, u32[]{:S(2)}, u32[]{:S(2)}) collective-permute-start(bf16[128,2048]{1,0:T(8,128)(2,1)S(1)} %pad_maximum_fusion.1.refs_1_), channel_id=1, source_target_pairs={{0,8},{4,12},{16,24},{20,28},{1,9},{5,13},{17,25},{21,29},{2,10},{... | collective-permute-start | bytes 1572872 | tf_op jit(solution)/shard_map/ppermute | solution.py:30
  22.3 0.0 collective-permute-done.3.refs_1_
  22.3 1.3 %collective-permute-start.7 = (bf16[128,2048]{1,0:T(8,128)(2,1)S(1)}, bf16[128,2048]{1,0:T(8,128)(2,1)S(1)}, u32[]{:S(2)}, u32[]{:S(2)}) collective-permute-start(bf16[128,2048]{1,0:T(8,128)(2,1)S(1)} %collective-permute-done.2.refs_0_), channel_id=1, source_target_pairs={{24,16},{25,17},{26,18},{27,19}} | collective-permute-start | bytes 1572872 | tf_op jit(solution)/shard_map/ppermute | solution.py:30
  23.6 4.7 %collective-permute-done.5.refs_3_ = bf16[128,2048]{1,0:T(8,128)(2,1)S(1)} collective-permute-done((bf16[128,2048]{1,0:T(8,128)(2,1)S(1)}, bf16[128,2048]{1,0:T(8,128)(2,1)S(1)}, u32[]{:S(2)}, u32[]{:S(2)}) %collective-permute-start.5) | collective-permute-done | bytes 524320 | tf_op jit(solution)/shard_map/ppermute | solution.py:30
  28.3 0.7 %collective-permute-start.11 = (bf16[128,2048]{1,0:T(8,128)(2,1)S(1)}, bf16[128,2048]{1,0:T(8,128)(2,1)S(1)}, u32[]{:S(2)}, u32[]{:S(2)}) collective-permute-start(bf16[128,2048]{1,0:T(8,128)(2,1)S(1)} %collective-permute-done.3.refs_1_), channel_id=1, source_target_pairs={{28,24},{29,25},{30,26},{31,27}} | collective-permute-start | bytes 1572872 | tf_op jit(solution)/shard_map/ppermute | solution.py:30
  29.0 0.0 collective-permute-done.6.refs_4_
  29.0 1.3 %collective-permute-start.13 = (bf16[128,2048]{1,0:T(8,128)(2,1)S(1)}, bf16[128,2048]{1,0:T(8,128)(2,1)S(1)}, u32[]{:S(2)}, u32[]{:S(2)}) collective-permute-start(bf16[128,2048]{1,0:T(8,128)(2,1)S(1)} %collective-permute-done.3.refs_1_), channel_id=1, source_target_pairs={{24,16},{28,20},{25,17},{29,21},{26,18},{30,22},{27,19},{31,23}} | collective-permute-start | bytes 1572872 | tf_op jit(solution)/shard_map/ppermute | solution.py:30
  30.3 2.0 %collective-permute-done.4.refs_2_ = bf16[128,2048]{1,0:T(8,128)(2,1)S(1)} collective-permute-done((bf16[128,2048]{1,0:T(8,128)(2,1)S(1)}, bf16[128,2048]{1,0:T(8,128)(2,1)S(1)}, u32[]{:S(2)}, u32[]{:S(2)}) %collective-permute-start.4) | collective-permute-done | bytes 524320 | tf_op jit(solution)/shard_map/ppermute | solution.py:30
  32.3 1.3 %collective-permute-start.10 = (bf16[128,2048]{1,0:T(8,128)(2,1)S(1)}, bf16[128,2048]{1,0:T(8,128)(2,1)S(1)}, u32[]{:S(2)}, u32[]{:S(2)}) collective-permute-start(bf16[128,2048]{1,0:T(8,128)(2,1)S(1)} %collective-permute-done.5.refs_3_), channel_id=1, source_target_pairs={{20,16},{21,17},{22,18},{23,19}} | collective-permute-start | bytes 1572872 | tf_op jit(solution)/shard_map/ppermute | solution.py:30
  33.6 0.0 collective-permute-done.12.refs_0_
  33.6 1.3 %collective-permute-start.8 = (bf16[128,2048]{1,0:T(8,128)(2,1)S(1)}, bf16[128,2048]{1,0:T(8,128)(2,1)S(1)}, u32[]{:S(2)}, u32[]{:S(2)}) collective-permute-start(bf16[128,2048]{1,0:T(8,128)(2,1)S(1)} %collective-permute-done.6.refs_4_), channel_id=1, source_target_pairs={{8,12},{12,8},{24,28},{28,24},{20,16},{9,13},{13,9},{25,29},{29,25... | collective-permute-start | bytes 1572872 | tf_op jit(solution)/shard_map/ppermute | solution.py:30
  34.9 0.0 collective-permute-done.7.refs_5_
  34.9 3.1 %collective-permute-start.9 = (bf16[128,2048]{1,0:T(8,128)(2,1)S(1)}, bf16[128,2048]{1,0:T(8,128)(2,1)S(1)}, u32[]{:S(2)}, u32[]{:S(2)}) collective-permute-start(bf16[128,2048]{1,0:T(8,128)(2,1)S(1)} %collective-permute-done.7.refs_5_), channel_id=1, source_target_pairs={{16,20},{17,21},{18,22},{19,23}} | collective-permute-start | bytes 1572872 | tf_op jit(solution)/shard_map/ppermute | solution.py:30
  38.0 0.0 collective-permute-done.11.refs_9_
  38.1 0.7 %collective-permute-start.14 = (bf16[128,2048]{1,0:T(8,128)(2,1)S(1)}, bf16[128,2048]{1,0:T(8,128)(2,1)S(1)}, u32[]{:S(2)}, u32[]{:S(2)}) collective-permute-start(bf16[128,2048]{1,0:T(8,128)(2,1)S(1)} %collective-permute-done.12.refs_0_), channel_id=1, source_target_pairs={{8,12},{12,8},{24,28},{28,24},{9,13},{13,9},{25,29},{29,25},{10,14... | collective-permute-start | bytes 1572872 | tf_op jit(solution)/shard_map/ppermute | solution.py:30
  38.8 5.8 %collective-permute-done.13.refs_1_ = bf16[128,2048]{1,0:T(8,128)(2,1)S(1)} collective-permute-done((bf16[128,2048]{1,0:T(8,128)(2,1)S(1)}, bf16[128,2048]{1,0:T(8,128)(2,1)S(1)}, u32[]{:S(2)}, u32[]{:S(2)}) %collective-permute-start.13) | collective-permute-done | bytes 524320 | tf_op jit(solution)/shard_map/ppermute | solution.py:30
  44.6 1.9 %collective-permute-start.15 = (bf16[128,2048]{1,0:T(8,128)(2,1)S(1)}, bf16[128,2048]{1,0:T(8,128)(2,1)S(1)}, u32[]{:S(2)}, u32[]{:S(2)}) collective-permute-start(bf16[128,2048]{1,0:T(8,128)(2,1)S(1)} %collective-permute-done.13.refs_1_), channel_id=1, source_target_pairs={{16,20},{20,16},{17,21},{21,17},{18,22},{22,18},{19,23},{23,19}} | collective-permute-start | bytes 1572872 | tf_op jit(solution)/shard_map/ppermute | solution.py:30
  46.5 0.0 copy-done
  46.5 0.0 copy-done.1
  46.5 4.3 %shard_map.46 = (f32[8,2,512,256]{3,2,1,0:T(8,128)S(1)}, f32[8,2,512,128]{3,2,1,0:T(8,128)S(1)}) custom-call(s32[6]{0:T(128)S(1)} %copy-done.1, bf16[256,4096]{1,0:T(8,128)(2,1)S(1)} %copy-done, bf16[128,2048]{1,0:T(8,128)(2,1)S(1)} %pad_maximum_fusion.refs_0_, bf16[128,2048]{1,0:T(8,128)(2,1)S(1)} %pad_maximum_fusion.1.refs_1_, ...), custom_call_target="tpu_custom_call" | custom-call | flops 1073741824 | bytes 8388608 | tf_op jit(solution)/shard_map/pallas_call | solution.py:381
  50.8 0.0 collective-permute-done.10.refs_8_
  50.8 0.0 collective-permute-done.8.refs_6_
  50.9 0.0 collective-permute-done.9.refs_7_
  50.9 7.8 %shard_map.47 = (f32[8,2,512,256]{3,2,1,0:T(8,128)S(1)}, f32[8,2,512,128]{3,2,1,0:T(8,128)S(1)}) custom-call(s32[6]{0:T(128)S(1)} %copy-done.1, bf16[256,4096]{1,0:T(8,128)(2,1)S(1)} %copy-done, f32[8,2,512,256]{3,2,1,0:T(8,128)S(1)} %get-tuple-element.9.old_mixed, ...), custom_call_target="tpu_custom_call", output_to_operand_aliasing={{0}: (2, {}), {1}: (3, {})} | custom-call | flops 1342177280 | bytes 8388608 | tf_op jit(solution)/shard_map/pallas_call | solution.py:381
  58.7 0.0 collective-permute-done.14.refs_2_
  58.7 0.0 collective-permute-done.15.refs_3_
  58.7 6.1 %shard_map.48 = bf16[256,4096]{1,0:T(8,128)(2,1)} custom-call(s32[6]{0:T(128)S(1)} %copy-done.1, bf16[256,4096]{1,0:T(8,128)(2,1)S(1)} %copy-done, f32[8,2,512,256]{3,2,1,0:T(8,128)S(1)} %get-tuple-element.11.mixed_ref, f32[8,2,512,128]{3,2,1,0:T(8,128)S(1)} %get-tuple-element.12.top_ref, bf16[128,2048]{1,0:T(8,128)(2,1)S(1)} %collective-permute-done.12.refs_0_, ...), custom_call_target="tpu_custom_call" | custom-call | flops 536870912 | bytes 8388608 | tf_op jit(solution)/shard_map/pallas_call | solution.py:381
  (2 shorter events, 0.1 us)
Async XLA Ops:
  0.0 46.5 %copy-start = (bf16[256,4096]{1,0:T(8,128)(2,1)S(1)}, bf16[256,4096]{1,0:T(8,128)(2,1)}, u32[]{:S(2)}) copy-start(bf16[256,4096]{1,0:T(8,128)(2,1)} %q_all.5) | copy-start | bytes 6291460
  0.0 46.5 %copy-start.1 = (s32[6]{0:T(128)S(1)}, s32[6]{0:T(128)}, u32[]{:S(2)}) copy-start(s32[6]{0:T(128)} %docs_ref.5) | copy-start | bytes 76
  1.5 5.9 %collective-permute-start.1 = (bf16[128,2048]{1,0:T(8,128)(2,1)S(1)}, bf16[128,2048]{1,0:T(8,128)(2,1)S(1)}, u32[]{:S(2)}, u32[]{:S(2)}) collective-permute-start(bf16[128,2048]{1,0:T(8,128)(2,1)S(1)} %pad_maximum_fusion.1.refs_1_), channel_id=1, source_target_pairs={{0,4},{8,12},{16,20},{24,28},{1,5},{9,13},{17,21},{25,29},{2,6},{1... | collective-permute-start | bytes 1572872 | tf_op jit(solution)/shard_map/ppermute | solution.py:30
  3.3 8.1 %collective-permute-start = (bf16[128,2048]{1,0:T(8,128)(2,1)S(1)}, bf16[128,2048]{1,0:T(8,128)(2,1)S(1)}, u32[]{:S(2)}, u32[]{:S(2)}) collective-permute-start(bf16[128,2048]{1,0:T(8,128)(2,1)S(1)} %pad_maximum_fusion.refs_0_), channel_id=1, source_target_pairs={{0,4},{8,12},{16,20},{24,28},{1,5},{9,13},{17,21},{25,29},{2,6},{1... | collective-permute-start | bytes 1572872 | tf_op jit(solution)/shard_map/ppermute | solution.py:30
  4.6 8.1 %collective-permute-start.2 = (bf16[128,2048]{1,0:T(8,128)(2,1)S(1)}, bf16[128,2048]{1,0:T(8,128)(2,1)S(1)}, u32[]{:S(2)}, u32[]{:S(2)}) collective-permute-start(bf16[128,2048]{1,0:T(8,128)(2,1)S(1)} %pad_maximum_fusion.refs_0_), channel_id=1, source_target_pairs={{12,24},{13,25},{14,26},{15,27}} | collective-permute-start | bytes 1572872 | tf_op jit(solution)/shard_map/ppermute | solution.py:30
  5.3 17.0 %collective-permute-start.3 = (bf16[128,2048]{1,0:T(8,128)(2,1)S(1)}, bf16[128,2048]{1,0:T(8,128)(2,1)S(1)}, u32[]{:S(2)}, u32[]{:S(2)}) collective-permute-start(bf16[128,2048]{1,0:T(8,128)(2,1)S(1)} %pad_maximum_fusion.1.refs_1_), channel_id=1, source_target_pairs={{8,24},{12,28},{9,25},{13,29},{10,26},{14,30},{11,27},{15,31}} | collective-permute-start | bytes 1572872 | tf_op jit(solution)/shard_map/ppermute | solution.py:30
  6.0 22.3 %collective-permute-start.5 = (bf16[128,2048]{1,0:T(8,128)(2,1)S(1)}, bf16[128,2048]{1,0:T(8,128)(2,1)S(1)}, u32[]{:S(2)}, u32[]{:S(2)}) collective-permute-start(bf16[128,2048]{1,0:T(8,128)(2,1)S(1)} %pad_maximum_fusion.1.refs_1_), channel_id=1, source_target_pairs={{0,16},{4,20},{1,17},{5,21},{2,18},{6,22},{3,19},{7,23}} | collective-permute-start | bytes 1572872 | tf_op jit(solution)/shard_map/ppermute | solution.py:30
  7.3 21.7 %collective-permute-start.6 = (bf16[128,2048]{1,0:T(8,128)(2,1)S(1)}, bf16[128,2048]{1,0:T(8,128)(2,1)S(1)}, u32[]{:S(2)}, u32[]{:S(2)}) collective-permute-start(bf16[128,2048]{1,0:T(8,128)(2,1)S(1)} %pad_maximum_fusion.refs_0_), channel_id=1, source_target_pairs={{0,8},{4,12},{16,24},{20,28},{8,20},{1,9},{5,13},{17,25},{21,29},{... | collective-permute-start | bytes 1572872 | tf_op jit(solution)/shard_map/ppermute | solution.py:30
  11.4 20.9 %collective-permute-start.4 = (bf16[128,2048]{1,0:T(8,128)(2,1)S(1)}, bf16[128,2048]{1,0:T(8,128)(2,1)S(1)}, u32[]{:S(2)}, u32[]{:S(2)}) collective-permute-start(bf16[128,2048]{1,0:T(8,128)(2,1)S(1)} %pad_maximum_fusion.refs_0_), channel_id=1, source_target_pairs={{4,16},{5,17},{6,18},{7,19}} | collective-permute-start | bytes 1572872 | tf_op jit(solution)/shard_map/ppermute | solution.py:30
  12.7 20.9 %collective-permute-start.12 = (bf16[128,2048]{1,0:T(8,128)(2,1)S(1)}, bf16[128,2048]{1,0:T(8,128)(2,1)S(1)}, u32[]{:S(2)}, u32[]{:S(2)}) collective-permute-start(bf16[128,2048]{1,0:T(8,128)(2,1)S(1)} %pad_maximum_fusion.1.refs_1_), channel_id=1, source_target_pairs={{0,8},{4,12},{16,24},{20,28},{1,9},{5,13},{17,25},{21,29},{2,10},{... | collective-permute-start | bytes 1572872 | tf_op jit(solution)/shard_map/ppermute | solution.py:30
  22.3 12.6 %collective-permute-start.7 = (bf16[128,2048]{1,0:T(8,128)(2,1)S(1)}, bf16[128,2048]{1,0:T(8,128)(2,1)S(1)}, u32[]{:S(2)}, u32[]{:S(2)}) collective-permute-start(bf16[128,2048]{1,0:T(8,128)(2,1)S(1)} %collective-permute-done.2.refs_0_), channel_id=1, source_target_pairs={{24,16},{25,17},{26,18},{27,19}} | collective-permute-start | bytes 1572872 | tf_op jit(solution)/shard_map/ppermute | solution.py:30
  28.3 9.7 %collective-permute-start.11 = (bf16[128,2048]{1,0:T(8,128)(2,1)S(1)}, bf16[128,2048]{1,0:T(8,128)(2,1)S(1)}, u32[]{:S(2)}, u32[]{:S(2)}) collective-permute-start(bf16[128,2048]{1,0:T(8,128)(2,1)S(1)} %collective-permute-done.3.refs_1_), channel_id=1, source_target_pairs={{28,24},{29,25},{30,26},{31,27}} | collective-permute-start | bytes 1572872 | tf_op jit(solution)/shard_map/ppermute | solution.py:30
  29.0 15.6 %collective-permute-start.13 = (bf16[128,2048]{1,0:T(8,128)(2,1)S(1)}, bf16[128,2048]{1,0:T(8,128)(2,1)S(1)}, u32[]{:S(2)}, u32[]{:S(2)}) collective-permute-start(bf16[128,2048]{1,0:T(8,128)(2,1)S(1)} %collective-permute-done.3.refs_1_), channel_id=1, source_target_pairs={{24,16},{28,20},{25,17},{29,21},{26,18},{30,22},{27,19},{31,23}} | collective-permute-start | bytes 1572872 | tf_op jit(solution)/shard_map/ppermute | solution.py:30
  32.3 18.5 %collective-permute-start.10 = (bf16[128,2048]{1,0:T(8,128)(2,1)S(1)}, bf16[128,2048]{1,0:T(8,128)(2,1)S(1)}, u32[]{:S(2)}, u32[]{:S(2)}) collective-permute-start(bf16[128,2048]{1,0:T(8,128)(2,1)S(1)} %collective-permute-done.5.refs_3_), channel_id=1, source_target_pairs={{20,16},{21,17},{22,18},{23,19}} | collective-permute-start | bytes 1572872 | tf_op jit(solution)/shard_map/ppermute | solution.py:30
  33.6 17.2 %collective-permute-start.8 = (bf16[128,2048]{1,0:T(8,128)(2,1)S(1)}, bf16[128,2048]{1,0:T(8,128)(2,1)S(1)}, u32[]{:S(2)}, u32[]{:S(2)}) collective-permute-start(bf16[128,2048]{1,0:T(8,128)(2,1)S(1)} %collective-permute-done.6.refs_4_), channel_id=1, source_target_pairs={{8,12},{12,8},{24,28},{28,24},{20,16},{9,13},{13,9},{25,29},{29,25... | collective-permute-start | bytes 1572872 | tf_op jit(solution)/shard_map/ppermute | solution.py:30
  34.9 15.9 %collective-permute-start.9 = (bf16[128,2048]{1,0:T(8,128)(2,1)S(1)}, bf16[128,2048]{1,0:T(8,128)(2,1)S(1)}, u32[]{:S(2)}, u32[]{:S(2)}) collective-permute-start(bf16[128,2048]{1,0:T(8,128)(2,1)S(1)} %collective-permute-done.7.refs_5_), channel_id=1, source_target_pairs={{16,20},{17,21},{18,22},{19,23}} | collective-permute-start | bytes 1572872 | tf_op jit(solution)/shard_map/ppermute | solution.py:30
  38.1 20.6 %collective-permute-start.14 = (bf16[128,2048]{1,0:T(8,128)(2,1)S(1)}, bf16[128,2048]{1,0:T(8,128)(2,1)S(1)}, u32[]{:S(2)}, u32[]{:S(2)}) collective-permute-start(bf16[128,2048]{1,0:T(8,128)(2,1)S(1)} %collective-permute-done.12.refs_0_), channel_id=1, source_target_pairs={{8,12},{12,8},{24,28},{28,24},{9,13},{13,9},{25,29},{29,25},{10,14... | collective-permute-start | bytes 1572872 | tf_op jit(solution)/shard_map/ppermute | solution.py:30
  44.6 14.1 %collective-permute-start.15 = (bf16[128,2048]{1,0:T(8,128)(2,1)S(1)}, bf16[128,2048]{1,0:T(8,128)(2,1)S(1)}, u32[]{:S(2)}, u32[]{:S(2)}) collective-permute-start(bf16[128,2048]{1,0:T(8,128)(2,1)S(1)} %collective-permute-done.13.refs_1_), channel_id=1, source_target_pairs={{16,20},{20,16},{17,21},{21,17},{18,22},{22,18},{19,23},{23,19}} | collective-permute-start | bytes 1572872 | tf_op jit(solution)/shard_map/ppermute | solution.py:30
